TPU v7x, 512 devices: a whole 4x4x16 slice. The times are simulated.
512 devices in a mesh: seq: 8 (over x, core), tok: 64 (over z, y).
Axes of the slice: x: 4, y: 4, z: 16, core: 2. Of those that a mesh axis runs over, the one named last changes fastest.
Arguments:
- block_in: bfloat16 [8, 256, 1024], P('seq'), may hold values from -6 to 6
- accept: int32 [2, 8, 256], P(None, 'seq'), may hold values 0 or 1
- cache_len: int32 [8], P('seq'), may hold values from 8192 to 16384, as said below
- slot_page: int32 [8, 192], P('seq', 'tok'), may hold values from -1 to 127, as said below
- cache_kv: bfloat16 [8, 192, 128, 2048], P('seq', 'tok'), as said below
- w_query: bfloat16 [1024, 1024], P('seq', 'tok'), may hold values from -0.25 to 0.25
- w_key_value: bfloat16 [1024, 2048], P('seq', 'tok'), may hold values from -0.375 to 0.375
- w_out: bfloat16 [1024, 1024], P('seq', 'tok'), may hold values from -0.1875 to 0.1875
- gain_attn: float32 [1024], replicated, may hold values from 0.1 to 1.9
- w_up: bfloat16 [1024, 4096], P('seq', 'tok'), may hold values from -0.1875 to 0.1875
- w_down: bfloat16 [4096, 1024], P('tok', 'seq'), may hold values from -0.09375 to 0.09375
- gain_mlp: float32 [1024], replicated, may hold values from 0.1 to 1.9
Outputs:
- refined: bfloat16 [8, 256, 1024], P('seq')
Inputs may be any that keep to these rules, and one draw needn't show every extreme that they name: `cache_len`: one sequence has exactly 16384 cached tokens. `slot_page`: slots j * 3 to (j + 1) * 3 - 1 of a row are those of index j of tok. Each page 0 to ceil(cache_len[s] / 128) - 1 of sequence s is in exactly one slot of row s, every other slot holds -1, and in every row some index of tok has all 3 of its slots filled. `cache_kv`: finite values; entries of empty slots are arbitrary.
All inputs are finite; a program needn't handle non-finite values. No bound on the sum of `accept` on one device may be relied on, other than what follows from the above.
Results may differ from a plain program's by a relative error of at most 0.035.
The roundings to bfloat16 on the way count: a program that leaves them out, or rounds other values in their place, can miss the bound.
Values may be sent and summed in bfloat16 or wider, within the bound.
A program may use at most 64 MiB of HBM per device.

v0:
```python
import jax
import jax.numpy as jnp
from jax import lax
from jax.sharding import PartitionSpec as P

HEADS = 16
HEAD_DIM = 64


EPSILON = 1e-05
FLOOR_SCORE = -1e30


def layer_norm(values, gain_vec):
    average = jnp.mean(values, axis=-1, keepdims=True)
    centered = values - average
    variance = jnp.mean(centered * centered, axis=-1, keepdims=True)
    return centered * lax.rsqrt(variance + EPSILON) * gain_vec


def merge_state(earlier, later):
    overall = jnp.maximum(earlier[0], later[0])
    early_factor = jnp.exp(earlier[0] - overall)
    late_factor = jnp.exp(later[0] - overall)
    totals = earlier[1] * early_factor + later[1] * late_factor
    weighted = earlier[2] * early_factor[..., None] + later[2] * late_factor[..., None]
    return (overall, totals, weighted)


def page_partial(queries, page_keys, page_values, usable):
    scores = jnp.einsum(
        "sqhe,skhe->sqhk", queries, page_keys, preferred_element_type=jnp.float32
    ) * HEAD_DIM ** (-0.5)
    masked = jnp.where(usable[:, None, None, :], scores, FLOOR_SCORE)
    peaks = jnp.max(masked, axis=-1)
    weights = jnp.where(usable[:, None, None, :], jnp.exp(masked - peaks[..., None]), 0.0).astype(
        jnp.bfloat16
    )
    weighted = jnp.einsum(
        "sqhk,skhe->sqhe", weights, page_values, preferred_element_type=jnp.float32
    )
    totals = jnp.sum(weights.astype(jnp.float32), axis=-1)
    return (peaks, totals, weighted)


def shards(
    block_in,
    accept,
    cache_len,
    slot_page,
    cache_kv,
    w_query,
    w_key_value,
    w_out,
    gain_attn,
    w_up,
    w_down,
    gain_mlp,
):
    groups, block_len, model_width = block_in.shape
    tok_parts = lax.axis_size("tok")
    tok_dev = block_len // tok_parts
    slot_count = cache_kv.shape[1]
    page_len = cache_kv.shape[2]
    own_index = lax.axis_index("tok")
    rows_q, rows_kv, rows_o, rows_up, cols_down = (
        lax.all_gather(w_query, "seq", axis=0, tiled=True),
        lax.all_gather(w_key_value, "seq", axis=0, tiled=True),
        lax.all_gather(w_out, "seq", axis=0, tiled=True),
        lax.all_gather(w_up, "seq", axis=0, tiled=True),
        lax.all_gather(w_down, "seq", axis=1, tiled=True),
    )
    full_q, full_kv, full_o = (
        lax.all_gather(rows_q, "tok", axis=1, tiled=True),
        lax.all_gather(rows_kv, "tok", axis=1, tiled=True),
        lax.all_gather(rows_o, "tok", axis=1, tiled=True),
    )

    def attend(inputs):
        flat_all = inputs.reshape(groups * block_len, model_width)
        own_rows = lax.dynamic_slice_in_dim(inputs, own_index * tok_dev, tok_dev, 1)
        flat_rows = own_rows.reshape(groups * tok_dev, model_width)
        queries = jnp.dot(flat_all, full_q, preferred_element_type=jnp.float32).astype(jnp.bfloat16)
        own_pair = jnp.dot(flat_rows, full_kv, preferred_element_type=jnp.float32).astype(
            jnp.bfloat16
        )
        own_pair = own_pair.reshape(groups, tok_dev, 2 * model_width)
        queries = queries.reshape(groups, block_len, HEADS, HEAD_DIM)
        own_keys = own_pair[..., :model_width].reshape(groups, tok_dev, HEADS, HEAD_DIM)
        own_values = own_pair[..., model_width:].reshape(groups, tok_dev, HEADS, HEAD_DIM)
        carry_state = page_partial(
            queries, own_keys, own_values, jnp.ones((groups, tok_dev), dtype=bool)
        )

        def slot_step(slot_index, carry_state):
            page_pair = lax.dynamic_index_in_dim(cache_kv, slot_index, 1, keepdims=False)
            page_no = lax.dynamic_index_in_dim(slot_page, slot_index, 1, keepdims=False)
            positions = page_no[:, None] * page_len + jnp.arange(page_len, dtype=jnp.int32)[None, :]
            usable = (page_no[:, None] >= 0) & (positions < cache_len[:, None])
            page_keys = page_pair[..., :model_width].reshape(groups, page_len, HEADS, HEAD_DIM)
            page_values = page_pair[..., model_width:].reshape(groups, page_len, HEADS, HEAD_DIM)
            return merge_state(carry_state, page_partial(queries, page_keys, page_values, usable))

        peaks, totals, weighted = lax.fori_loop(0, slot_count, slot_step, carry_state)
        peak_parts = lax.all_to_all(peaks[None], "tok", split_axis=2, concat_axis=0, tiled=True)
        total_parts = lax.all_to_all(totals[None], "tok", split_axis=2, concat_axis=0, tiled=True)
        weighted_parts = lax.all_to_all(
            weighted.reshape(groups, block_len, model_width)[None],
            "tok",
            split_axis=2,
            concat_axis=0,
            tiled=True,
        )
        overall = jnp.max(peak_parts, axis=0)
        factor = jnp.exp(peak_parts - overall[None])
        denominator = jnp.sum(total_parts * factor, axis=0)
        split_parts = weighted_parts.reshape(weighted_parts.shape[:-1] + (HEADS, HEAD_DIM))
        numerator = jnp.sum(split_parts * factor[..., None], axis=0)
        attention = (numerator / denominator[..., None]).reshape(
            numerator.shape[:-2] + (model_width,)
        )
        attention = attention.astype(jnp.bfloat16).reshape(groups * tok_dev, model_width)
        residual = flat_rows.astype(jnp.float32) + jnp.dot(
            attention, full_o, preferred_element_type=jnp.float32
        )
        return (
            layer_norm(residual, gain_attn)
            .astype(jnp.bfloat16)
            .reshape(groups, tok_dev, model_width)
        )

    def feed(settled):
        products = jnp.einsum(
            "gtd,df->gtf",
            lax.all_gather(settled, "tok", axis=1, tiled=True),
            rows_up,
            preferred_element_type=jnp.float32,
        )
        hidden = jax.nn.gelu(products, approximate=False).astype(jnp.bfloat16)
        mlp_term = jnp.einsum("gtf,fd->gtd", hidden, cols_down, preferred_element_type=jnp.float32)
        projected = lax.psum_scatter(mlp_term, "tok", scatter_dimension=1, tiled=True)
        finished = layer_norm(settled.astype(jnp.float32) + projected, gain_mlp).astype(
            jnp.bfloat16
        )
        return lax.all_gather(finished, "tok", axis=1, tiled=True)

    first_out = feed(attend(block_in))
    second_in = jnp.where(accept[0][..., None] == 1, first_out, block_in)
    second_out = feed(attend(second_in))
    return jnp.where(accept[1][..., None] == 1, second_out, second_in)


def solution(mesh):
    in_specs = (
        P("seq", None, None),
        P(None, "seq", None),
        P("seq"),
        P("seq", "tok"),
        P("seq", "tok", None, None),
        P("seq", "tok"),
        P("seq", "tok"),
        P("seq", "tok"),
        P(),
        P("seq", "tok"),
        P("tok", "seq"),
        P(),
    )
    out_specs = P("seq", None, None)
    return jax.shard_map(shards, mesh=mesh, in_specs=in_specs, out_specs=out_specs, check_vma=False)
```

profile of v0, /device:TPU:2, one launch (start us, length us, event | category | flops | bytes accessed | tf_op | source)
XLA Modules:
  0.0 1601.0 jit_solution(3491275169055620532)
XLA Ops:
  6.5 16.2 %all_gather.38 = bf16[1024,16]{0,1:T(8,128)(2,1)} all-gather(bf16[128,16]{0,1:T(8,128)(2,1)} %param.21), channel_id=1, replica_groups=mesh['seq'=8,'tok'=64] {'seq'}, dimensions={0}, use_global_device_ids=true | all-gather | bytes 36864 | tf_op jit(solution)/shard_map/all_gather | solution.py:67
  22.9 13.1 all_gather.36
  38.0 126.6 %all-gather.10.cloned.1.call-done = bf16[1024,1024]{0,1:T(8,128)(2,1)} async-done(((bf16[1024,16]{0,1:T(8,128)(2,1)}), bf16[1024,1024]{0,1:T(8,128)(2,1)}) %all-gather.10.cloned.1.call-update) | async-done | bytes 2097168 | tf_op jit(solution)/shard_map/all_gather | solution.py:74
  167.1 143.0 %all-gather.8.cloned.1.call-done = bf16[1024,2048]{0,1:T(8,128)(2,1)} async-done(((bf16[1024,32]{0,1:T(8,128)(2,1)}), bf16[1024,2048]{0,1:T(8,128)(2,1)}) %all-gather.8.cloned.1.call-update) | async-done | bytes 4194320 | tf_op jit(solution)/shard_map/all_gather | solution.py:75
  310.1 3.4 fusion.32
  314.3 14.3 while.34
  329.3 8.9 all-to-all-start.1
  339.0 15.4 all-to-all-done.1
  354.4 4.6 all-to-all-start.2
  361.0 14.3 all-to-all-done.2
  375.3 5.5 all-to-all-start
  380.9 12.7 all_gather.40
  393.6 11.0 all_gather.43
  404.6 11.2 all_gather.44
  420.9 4.6 all-to-all-done
  425.5 3.1 multiply_reduce_fusion.1
  428.6 106.4 %all-gather.12.cloned.1.call-done = bf16[1024,1024]{0,1:T(8,128)(2,1)} async-done(((bf16[1024,16]{0,1:T(8,128)(2,1)}), bf16[1024,1024]{0,1:T(8,128)(2,1)}) %all-gather.12.cloned.1.call-update) | async-done | bytes 2097168 | tf_op jit(solution)/shard_map/all_gather | solution.py:76
  537.6 98.1 %all-gather.2 = bf16[64,4,1024]{2,1,0:T(4,128)(2,1)S(1)} all-gather(bf16[1,4,1024]{2,1,0:T(4,128)(2,1)S(1)} %fusion.126), channel_id=2, replica_groups=mesh['seq'=8,'tok'=64] {'tok'}, dimensions={0}, use_global_device_ids=true | all-gather | bytes 532480 | tf_op jit(solution)/shard_map/all_gather | solution.py:135
  636.7 3.0 convolution_bitcast_fusion.4
  641.7 266.9 %all-reduce.5.cloned.1.call-done = f32[1,256,1024]{2,1,0:T(8,128)} async-done(((f32[1,256,1024]{2,1,0:T(8,128)}), f32[1,256,1024]{2,1,0:T(8,128)}) %all-reduce.5.cloned.1.call-update) | async-done | bytes 1048592
  911.5 98.7 %all_gather.45 = bf16[1,256,1024]{2,0,1:T(2,128)(2,1)S(1)} all-gather(bf16[1,4,1024]{2,0,1:T(2,128)(2,1)S(1)} %copy.77), channel_id=1, replica_groups=mesh['seq'=8,'tok'=64] {'tok'}, dimensions={1}, use_global_device_ids=true | all-gather | bytes 532480 | tf_op jit(solution)/shard_map/all_gather | solution.py:145
  1011.5 3.4 fusion.33
  1015.7 14.5 while.35
  1030.9 10.5 all-to-all-start.4
  1042.2 15.4 all-to-all-done.4
  1057.6 5.9 all-to-all-start.5
  1065.5 16.6 %all-to-all-done.5 = f32[1,1,256,16]{3,1,0,2:T(1,128)S(1)} async-done(((f32[1,1,256,16]{3,1,0,2:T(1,128)}), f32[1,1,256,16]{3,1,0,2:T(1,128)S(1)}, u32[]{:S(2)}, u32[]{:S(2)}) %all-to-all-start.5) | async-done | bytes 16416 | tf_op jit(solution)/shard_map/all_to_all | solution.py:106
  1082.1 5.0 all-to-all-start.3
  1092.5 28.2 %all-to-all-done.3 = f32[1,1,256,1024]{3,1,0,2:T(1,128)S(1)} async-done(((f32[1,1,256,1024]{3,1,0,2:T(1,128)}), f32[1,1,256,1024]{3,1,0,2:T(1,128)S(1)}, u32[]{:S(2)}, u32[]{:S(2)}) %all-to-all-start.3) | async-done | bytes 1048608 | tf_op jit(solution)/shard_map/all_to_all | solution.py:107
  1125.4 99.8 %all-gather.3 = bf16[64,4,1024]{2,1,0:T(4,128)(2,1)S(1)} all-gather(bf16[1,4,1024]{2,1,0:T(4,128)(2,1)S(1)} %fusion.127), channel_id=3, replica_groups=mesh['seq'=8,'tok'=64] {'tok'}, dimensions={0}, use_global_device_ids=true | all-gather | bytes 532480 | tf_op jit(solution)/shard_map/all_gather | solution.py:135
  1227.3 265.2 %all-reduce.7.cloned.1.call-done = f32[1,256,1024]{2,1,0:T(8,128)} async-done(((f32[1,256,1024]{2,1,0:T(8,128)}), f32[1,256,1024]{2,1,0:T(8,128)}) %all-reduce.7.cloned.1.call-update) | async-done | bytes 1048592
  1495.3 98.1 %all_gather.47 = bf16[1,256,1024]{2,0,1:T(2,128)(2,1)S(1)} all-gather(bf16[1,4,1024]{2,0,1:T(2,128)(2,1)S(1)} %copy.87), channel_id=1, replica_groups=mesh['seq'=8,'tok'=64] {'tok'}, dimensions={1}, use_global_device_ids=true | all-gather | bytes 532480 | tf_op jit(solution)/shard_map/all_gather | solution.py:145
  (163 shorter events, 68.0 us)
Async XLA Ops:
  6.5 158.0 %copy-start.2 = (bf16[1,256,1024]{2,1,0:T(8,128)(2,1)S(1)}, bf16[1,256,1024]{2,1,0:T(8,128)(2,1)}, u32[]{:S(2)}) copy-start(bf16[1,256,1024]{2,1,0:T(8,128)(2,1)} %param.16) | copy-start | bytes 1572868
  6.5 158.0 %all-gather.10.cloned.1.call-start = ((), (), s32[]{:S(2)}) async-start(), calls=%async_computation.7 | async-start | bytes 2129920 | tf_op jit(solution)/shard_map/all_gather | solution.py:74
  22.8 287.3 %all-gather.8.cloned.1.call-start = ((), (), s32[]{:S(2)}) async-start(), calls=%async_computation.6 | async-start | bytes 4259840 | tf_op jit(solution)/shard_map/all_gather | solution.py:75
  167.1 147.2 %copy-start.5 = (s32[1,3]{1,0:T(1,128)S(1)}, s32[1,3]{1,0:T(1,128)}, u32[]{:S(2)}) copy-start(s32[1,3]{1,0:T(1,128)} %param.19) | copy-start | bytes 40
  329.3 25.0 %all-to-all-start.1 = ((f32[1,1,256,16]{3,1,0,2:T(1,128)}), f32[1,1,256,16]{3,1,0,2:T(1,128)S(1)}, u32[]{:S(2)}, u32[]{:S(2)}) async-start(f32[1,1,256,16]{3,1,0,2:T(1,128)} %bitcast.47), calls=%async_computation.1 | async-start | bytes 262144 | tf_op jit(solution)/shard_map/all_to_all | solution.py:105
  354.4 20.9 %all-to-all-start.2 = ((f32[1,1,256,16]{3,1,0,2:T(1,128)}), f32[1,1,256,16]{3,1,0,2:T(1,128)S(1)}, u32[]{:S(2)}, u32[]{:S(2)}) async-start(f32[1,1,256,16]{3,1,0,2:T(1,128)} %bitcast.49), calls=%async_computation.2 | async-start | bytes 262144 | tf_op jit(solution)/shard_map/all_to_all | solution.py:106
  359.0 21.9 %copy-start.9 = (bf16[128,16]{0,1:T(8,128)(2,1)S(1)}, bf16[128,16]{0,1:T(8,128)(2,1)}, u32[]{:S(2)}) copy-start(bf16[128,16]{0,1:T(8,128)(2,1)} %param.23) | copy-start | bytes 12292
  359.0 34.6 %copy-start.6 = (bf16[128,64]{0,1:T(8,128)(2,1)S(1)}, bf16[128,64]{0,1:T(8,128)(2,1)}, u32[]{:S(2)}) copy-start(bf16[128,64]{0,1:T(8,128)(2,1)} %param.25) | copy-start | bytes 49156
  359.0 45.6 %copy-start.7 = (bf16[64,128]{1,0:T(8,128)(2,1)S(1)}, bf16[64,128]{1,0:T(8,128)(2,1)}, u32[]{:S(2)}) copy-start(bf16[64,128]{1,0:T(8,128)(2,1)} %param.26) | copy-start | bytes 49156
  375.3 50.2 %all-to-all-start = ((f32[1,1,256,1024]{3,1,0,2:T(1,128)}), f32[1,1,256,1024]{3,1,0,2:T(1,128)}, u32[]{:S(2)}, u32[]{:S(2)}) async-start(f32[1,1,256,1024]{3,1,0,2:T(1,128)} %copy.74), calls=%async_computation | async-start | bytes 2097152 | tf_op jit(solution)/shard_map/all_to_all | solution.py:107
  380.8 154.2 %all-gather.12.cloned.1.call-start = ((), (), s32[]{:S(2)}) async-start(), calls=%async_computation.8 | async-start | bytes 2129920 | tf_op jit(solution)/shard_map/all_gather | solution.py:76
  393.5 515.0 %all-reduce.5.cloned.1.call-start = ((), (), s32[]{:S(2)}) async-start(), calls=%async_computation.9 | async-start | bytes 2097152
  418.2 116.8 %copy-start.3 = (bf16[1,256,1024]{2,1,0:T(8,128)(2,1)S(1)}, bf16[1,256,1024]{2,1,0:T(8,128)(2,1)}, u32[]{:S(2)}) copy-start(bf16[1,256,1024]{2,1,0:T(8,128)(2,1)} %param.16) | copy-start | bytes 1572868
  425.5 112.1 %copy-start.4 = (f32[1024]{0:T(1024)S(1)}, f32[1024]{0:T(1024)}, u32[]{:S(2)}) copy-start(f32[1024]{0:T(1024)} %param.24) | copy-start | bytes 12292
  635.8 5.9 copy-start.10
  635.8 274.8 %copy-start.8 = (f32[1024]{0:T(1024)S(1)}, f32[1024]{0:T(1024)}, u32[]{:S(2)}) copy-start(f32[1024]{0:T(1024)} %param.27) | copy-start | bytes 12292
  908.5 101.9 %copy-start.11 = (bf16[1024,1024]{0,1:T(8,128)(2,1)S(1)}, bf16[1024,1024]{0,1:T(8,128)(2,1)}, u32[]{:S(2)}) copy-start(bf16[1024,1024]{0,1:T(8,128)(2,1)} %all-gather.10.cloned.1.call-done) | copy-start | bytes 6291460
  1010.4 1.0 copy-start
  1030.9 26.7 %all-to-all-start.4 = ((f32[1,1,256,16]{3,1,0,2:T(1,128)}), f32[1,1,256,16]{3,1,0,2:T(1,128)S(1)}, u32[]{:S(2)}, u32[]{:S(2)}) async-start(f32[1,1,256,16]{3,1,0,2:T(1,128)} %bitcast.70), calls=%async_computation.4 | async-start | bytes 262144 | tf_op jit(solution)/shard_map/all_to_all | solution.py:105
  1057.6 24.5 %all-to-all-start.5 = ((f32[1,1,256,16]{3,1,0,2:T(1,128)}), f32[1,1,256,16]{3,1,0,2:T(1,128)S(1)}, u32[]{:S(2)}, u32[]{:S(2)}) async-start(f32[1,1,256,16]{3,1,0,2:T(1,128)} %bitcast.72), calls=%async_computation.5 | async-start | bytes 262144 | tf_op jit(solution)/shard_map/all_to_all | solution.py:106
  1082.1 38.6 %all-to-all-start.3 = ((f32[1,1,256,1024]{3,1,0,2:T(1,128)}), f32[1,1,256,1024]{3,1,0,2:T(1,128)S(1)}, u32[]{:S(2)}, u32[]{:S(2)}) async-start(f32[1,1,256,1024]{3,1,0,2:T(1,128)} %copy.84), calls=%async_computation.3 | async-start | bytes 2097152 | tf_op jit(solution)/shard_map/all_to_all | solution.py:107
  1087.1 405.4 %all-reduce.7.cloned.1.call-start = ((), (), s32[]{:S(2)}) async-start(), calls=%async_computation.10 | async-start | bytes 2097152
  1089.8 33.0 %copy-start.1 = (bf16[1,256,1024]{2,1,0:T(8,128)(2,1)S(1)}, bf16[1,256,1024]{2,1,0:T(8,128)(2,1)}, u32[]{:S(2)}) copy-start(bf16[1,256,1024]{2,1,0:T(8,128)(2,1)} %copy-done) | copy-start | bytes 1572868
Sparse Core Ops, SparseCore 0:
  22.9 141.5 all-gather.9
  167.5 142.5 all-gather.7
  393.7 141.2 all-gather.11
  639.8 268.6 all-reduce.4
  1227.5 265.0 all-reduce.6
where the time goes:
time: 1600 us
  waiting for transfers between devices  1000 us (62%)
  blocking collectives  459 us (29%)
  starting transfers between devices  40.8 us (3%)
  matrix products  29.6 us (2%)
  other arithmetic  28.5 us (2%)
  local copies, waits for them, and re-layouts  22.3 us (1%)
    unnamed x7, waiting for transfers between devices  532 us
    all_gather x2, blocking collectives, feed(): lax.all_gather(settled, 'tok', axis=1, tiled=True)  198 us
    all_gather x2, blocking collectives, feed(): return lax.all_gather(finished, 'tok', axis=1, tiled=True)  197 us
    all_gather x1, waiting for transfers between devices, shards(): lax.all_gather(rows_kv, 'tok', axis=1, tiled=True)  143 us
    all_gather x1, waiting for transfers between devices, shards(): lax.all_gather(rows_q, 'tok', axis=1, tiled=True)  127 us
    all_gather x1, waiting for transfers between devices, shards(): lax.all_gather(rows_o, 'tok', axis=1, tiled=True)  106 us
    all_to_all x2, waiting for transfers between devices, attend(): lax.all_to_all(weighted.reshape(groups, block_len, model_width)[None], 't...  32.7 us
  transfers between devices with their start and end apart: 11, of which 11 were waited for; matrix products, arithmetic and copies ran while one was open for 2% of the time, Pallas kernels for 0%

commit v1 on v0

v1 whole, which is shorter than its diff:
```python
import jax
import jax.numpy as jnp
from jax import lax
from jax.experimental import pallas as pl
from jax.experimental.pallas import tpu as pltpu
from jax.sharding import PartitionSpec as P

MESH = pl.DeviceIdType.MESH
BF = jnp.bfloat16
F32 = jnp.float32

D = 1024
TOK = 256
NZ, NY, NX = 16, 4, 4
ROWS = TOK // NZ
KEYS = 384
EPSILON = 1e-05
FLOOR_SCORE = -1e30
MASKED = -3e38

(WS, AZ, KVY, OY, QX, KVX, OX, QC, KVC, OC, UZ, DZ, UX, DX, UC, DC) = range(16)
(GQZ, GQY, RSY, RSYM, RSZ, RSZM, GAY, GOY, RFY) = range(9)
FIN_Z, FIN_Y = 34, 35
N_SEM = 36


def dot_nn(a, b):
    return lax.dot_general(a, b, (((1,), (0,)), ((), ())), preferred_element_type=F32)


def dot_nt(a, b):
    return lax.dot_general(a, b, (((1,), (1,)), ((), ())), preferred_element_type=F32)


def layer_norm(values, gain):
    average = jnp.mean(values, axis=-1, keepdims=True)
    centered = values - average
    variance = jnp.mean(centered * centered, axis=-1, keepdims=True)
    return centered * lax.rsqrt(variance + EPSILON) * gain


def kernel(
    x_ref, accept_ref, len_ref, page_ref, cache_ref, wq_ref, wkv_ref, wo_ref, wu_ref, wd_ref, ga_ref, gm_ref,
    out_ref,
    kv_c, vt, ws, az, qw, kvw, ow, up, down,
    q_own, qz, qt, ot, ml, ry, rym, tz, ml2, rz, rzm, wt, att, ob, fp, fin, fz,
    ssem, rsem, lsem,
):
    s, t = lax.axis_index("seq"), lax.axis_index("tok")
    x, c = lax.div(s, 2), lax.rem(s, 2)
    z, y = lax.div(t, NY), lax.rem(t, NY)
    za, zb, zc = lax.div(z, 8), lax.div(lax.rem(z, 8), 2), lax.rem(z, 2)

    def dev_z(k):
        zp = lax.rem(z + k, NZ)
        return zp, {"seq": s, "tok": zp * NY + y}

    def dev_y(k):
        yp = lax.rem(y + k, NY)
        return yp, {"seq": s, "tok": z * NY + yp}

    def dev_s(k):
        return {"seq": lax.rem(s + k, 2 * NX), "tok": t}

    def dev_x(k):
        return {"seq": lax.rem(x + k, NX) * 2 + c, "tok": t}

    partner = {"seq": x * 2 + 1 - c, "tok": t}

    def put(src, dst, ph, dev):
        return pltpu.make_async_remote_copy(
            src_ref=src, dst_ref=dst, send_sem=ssem.at[ph], recv_sem=rsem.at[ph], device_id=dev, device_id_type=MESH
        )

    def arrived(view, ph):
        put(view, view, ph, partner).wait_recv()

    def sent(view, ph):
        put(view, view, ph, partner).wait_send()

    cache_copy = pltpu.make_async_copy(cache_ref, kv_c, lsem)
    cache_copy.start()
    az[za, zb, zc, 0:16, :] = wq_ref[...]
    az[za, zb, zc, 16:48, :] = wkv_ref[...]
    az[za, zb, zc, 48:64, :] = wo_ref[...]
    ws[s] = wq_ref[...]
    up[x, c, z] = wu_ref[...]
    down[x, c, z] = wd_ref[...]
    barrier = pltpu.get_barrier_semaphore()
    for k in range(1, 8):
        pl.semaphore_signal(barrier, inc=1, device_id=dev_s(k), device_id_type=MESH)
    for k in range(1, NY):
        pl.semaphore_signal(barrier, inc=1, device_id=dev_y(k)[1], device_id_type=MESH)

    @pl.loop(1, NZ)
    def _(k):
        pl.semaphore_signal(barrier, inc=1, device_id=dev_z(k)[1], device_id_type=MESH)

    pl.semaphore_wait(barrier, 7 + (NY - 1) + (NZ - 1))

    for k in range(1, 8):
        put(wq_ref, ws.at[s], WS, dev_s(k)).start()

    @pl.loop(1, NZ)
    def _(k):
        put(az.at[za, zb, zc], az.at[za, zb, zc], AZ, dev_z(k)[1]).start()

    arrived(ws.at[pl.ds(0, 7)], WS)
    wq_cols = jnp.concatenate([ws[i] for i in range(8)], axis=1)
    q_piece = dot_nt(wq_cols, x_ref[...]).astype(BF) * jnp.asarray(0.125, BF)
    qt[0, z, y] = q_piece

    @pl.loop(1, NZ)
    def _(k):
        put(qt.at[0, z, y], qt.at[0, z, y], 16 + GQZ, dev_z(k)[1]).start()

    @pl.loop(1, NZ)
    def _(k):
        put(wu_ref, up.at[x, c, z], UZ, dev_z(k)[1]).start()

    @pl.loop(1, NZ)
    def _(k):
        put(wd_ref, down.at[x, c, z], DZ, dev_z(k)[1]).start()

    cache_copy.wait()
    vt[:, 128:144, :] = jnp.ones((8, 16, KEYS), BF)

    @pl.loop(0, 8)
    def _(i):
        for j in range(3):
            piece = kv_c[j, :, pl.ds(pl.multiple_of(D + i * 128, 128), 128)]
            vt[i, 0:128, 128 * j : 128 * (j + 1)] = jnp.transpose(piece)

    arrived(qt.at[0, pl.ds(0, NZ - 1), 0], 16 + GQZ)
    for k in range(1, NY):
        put(qt.at[0, :, y], qt.at[0, :, y], 16 + GQY, dev_y(k)[1]).start()

    arrived(up.at[0, 0, pl.ds(0, NZ - 1)], AZ)
    for a in range(2):
        for d in range(2):
            kvw[x, c, a, d, y] = az[a, y, d, 16:48, :]
    for b in range(2):
        for d in range(2):
            ow[x, c, b, d, y] = az[lax.div(y, 2), 2 * lax.rem(y, 2) + b, d, 48:64, :]
    for k in range(1, NY):
        yp, dev = dev_y(k)
        put(az.at[:, yp, :, 16:48, :], kvw.at[x, c, :, :, y], KVY, dev).start()
        put(
            az.at[lax.div(yp, 2), pl.ds(2 * lax.rem(yp, 2), 2), :, 48:64, :], ow.at[x, c, :, :, y], OY, dev
        ).start()
    qw[x, c] = az[:, :, :, 0:16, :]
    for k in range(1, NX):
        put(qw.at[x, c], qw.at[x, c], QX, dev_x(k)).start()
    arrived(kvw.at[0, 0, :, :, pl.ds(0, 3)], KVY)
    arrived(ow.at[0, 0, :, :, pl.ds(0, 3)], OY)
    for k in range(1, NX):
        put(kvw.at[x, c], kvw.at[x, c], KVX, dev_x(k)).start()
        put(ow.at[x, c], ow.at[x, c], OX, dev_x(k)).start()

    length = len_ref[0]
    limits = [jnp.where(page_ref[0, j] >= 0, length - page_ref[0, j] * 128, 0) for j in range(3)]
    own_rows = pl.ds(pl.multiple_of(z * ROWS, ROWS), ROWS)
    current = x_ref[own_rows, :]

    for p in range(2):
        base = 16 + 9 * p
        if p == 1:
            arrived_q = jnp.concatenate([qw[i, j].reshape(256, 128) for i in range(4) for j in range(2)], axis=1)
            q_own[...] = dot_nt(current, arrived_q).astype(BF) * jnp.asarray(0.125, BF)
            qz[z] = q_own[...]

            @pl.loop(1, NZ)
            def _(k):
                put(q_own, qz.at[z], base + GQZ, dev_z(k)[1]).start()

            arrived(qz.at[pl.ds(0, NZ - 1)], base + GQZ)
            qt[1, :, y] = jnp.transpose(qz[...].reshape(TOK, 256)).reshape(NZ, 16, TOK)
            for k in range(1, NY):
                put(qt.at[1, :, y], qt.at[1, :, y], base + GQY, dev_y(k)[1]).start()
        arrived(qt.at[p, :, pl.ds(0, 3)], base + GQY)

        @pl.loop(0, NY)
        def _(j):
            g = lax.rem(y + 1 + j, NY)
            for i in range(2):
                keys = kv_c[:, :, pl.ds(pl.multiple_of(g * 256 + i * 128, 128), 128)].reshape(KEYS, 128)
                q_pair = qt[p, pl.ds(4 * g + 2 * i, 2)].reshape(2, 64, TOK)
                none = jnp.zeros((64, TOK), BF)
                both = jnp.concatenate(
                    [
                        jnp.concatenate([q_pair[0], none], axis=1),
                        jnp.concatenate([none, q_pair[1]], axis=1),
                    ],
                    axis=0,
                )
                scores = dot_nn(keys, both)
                offsets = lax.broadcasted_iota(jnp.int32, (128, 2 * TOK), 0)
                masked = jnp.concatenate(
                    [
                        jnp.where(offsets < limits[n], scores[128 * n : 128 * (n + 1)], MASKED)
                        for n in range(3)
                    ],
                    axis=0,
                )
                peaks = jnp.maximum(jnp.max(masked, axis=0, keepdims=True), FLOOR_SCORE)
                weights = jnp.exp(masked - peaks).astype(BF)
                summed = dot_nn(vt[2 * g + i], weights)
                ot[p, g, 128 * i : 128 * i + 64, :] = summed[0:64, 0:TOK].astype(BF)
                ot[p, g, 128 * i + 64 : 128 * i + 128, :] = summed[64:128, TOK : 2 * TOK].astype(BF)
                ml[p, g, 2 * i : 2 * i + 1, :] = peaks[:, 0:TOK]
                ml[p, g, 2 * i + 1 : 2 * i + 2, :] = peaks[:, TOK : 2 * TOK]
                ml[p, g, 4 + 2 * i : 5 + 2 * i, :] = summed[128:129, 0:TOK]
                ml[p, g, 5 + 2 * i : 6 + 2 * i, :] = summed[128:129, TOK : 2 * TOK]

            @pl.when(j < NY - 1)
            def _():
                dev = {"seq": s, "tok": z * NY + g}
                put(ot.at[p, g], ry.at[p, y], base + RSY, dev).start()
                put(ml.at[p, g], rym.at[p, y], base + RSYM, dev).start()

        ry[p, y] = ot[p, y]
        rym[p, y] = ml[p, y]
        if p == 0:
            arrived(qw.at[pl.ds(0, 3), 0], QX)
            arrived(kvw.at[pl.ds(0, 3), 0], KVX)
            arrived(ow.at[pl.ds(0, 3), 0], OX)
            put(kvw.at[:, c], kvw.at[:, c], KVC, partner).start()
            put(ow.at[:, c], ow.at[:, c], OC, partner).start()
            put(qw.at[:, c], qw.at[:, c], QC, partner).start()
            arrived(up.at[0, 0, pl.ds(0, NZ - 1)], UZ)
            for k in range(1, NX):
                put(up.at[x, c], up.at[x, c], UX, dev_x(k)).start()
            arrived(kvw.at[:, 0], KVC)

        w_pair = jnp.concatenate([kvw[i, j].reshape(512, 128) for i in range(4) for j in range(2)], axis=1)
        pair = dot_nt(current, w_pair)
        row_head = lax.div(lax.broadcasted_iota(jnp.int32, (64, 256), 0), 16)
        lane_head = lax.div(lax.broadcasted_iota(jnp.int32, (64, 256), 1), 64)
        own_head = row_head == lane_head
        k_block = jnp.where(own_head, jnp.concatenate([pair[:, 0:256]] * 4, axis=0), 0.0).astype(BF)
        v_block = jnp.where(own_head, jnp.concatenate([pair[:, 256:512]] * 4, axis=0), 0.0)
        q_heads = qt[p, pl.ds(4 * y, 4)].reshape(256, TOK)
        b_scores = dot_nn(k_block, q_heads).reshape(4, 16, TOK)
        b_peak = jnp.max(b_scores, axis=1)
        b_weights = jnp.exp(b_scores - b_peak[:, None, :]).astype(BF)
        b_total = jnp.sum(b_weights.astype(F32), axis=1)
        b_sum = dot_nn(jnp.transpose(v_block).astype(BF), b_weights.reshape(64, TOK))

        arrived(ry.at[p, pl.ds(0, 3)], base + RSY)
        arrived(rym.at[p, pl.ds(0, 3)], base + RSYM)
        peaks_y = rym[p, :, 0:4, :]
        peak = jnp.maximum(jnp.max(peaks_y, axis=0), b_peak)
        scale = jnp.exp(peaks_y - peak[None])
        b_scale = jnp.exp(b_peak - peak)
        total = jnp.sum(scale * rym[p, :, 4:8, :], axis=0) + b_scale * b_total
        ml2[p, 0:4, :] = peak
        ml2[p, 4:8, :] = total
        parts = []
        for h in range(4):
            rows = slice(64 * h, 64 * h + 64)
            value = b_sum[rows] * b_scale[h : h + 1]
            for i in range(NY):
                value += ry[p, i, rows, :].astype(F32) * scale[i, h : h + 1]
            parts.append(value)
        tz[p] = jnp.transpose(jnp.concatenate(parts, axis=0)).astype(BF).reshape(NZ, ROWS, 256)

        @pl.loop(1, NZ)
        def _(k):
            zp, dev = dev_z(k)
            half = pl.ds(pl.multiple_of(lax.div(zp, 8) * 128, 128), 128)
            put(tz.at[p, zp], rz.at[p, z], base + RSZ, dev).start()
            put(ml2.at[p, :, half], rzm.at[p, z], base + RSZM, dev).start()

        rz[p, z] = tz[p, z]
        rzm[p, z] = ml2[p, :, pl.ds(pl.multiple_of(za * 128, 128), 128)]
        if p == 0:
            arrived(down.at[0, 0, pl.ds(0, NZ - 1)], DZ)
            for k in range(1, NX):
                put(down.at[x, c], down.at[x, c], DX, dev_x(k)).start()
            arrived(ow.at[:, 0], OC)

        arrived(rz.at[p, pl.ds(0, NZ - 1)], base + RSZ)
        arrived(rzm.at[p, pl.ds(0, NZ - 1)], base + RSZM)
        peaks_z = rzm[p, :, 0:4, :]
        scale_z = jnp.exp(peaks_z - jnp.max(peaks_z, axis=0, keepdims=True))
        share = scale_z / jnp.sum(scale_z * rzm[p, :, 4:8, :], axis=0, keepdims=True)
        share = jnp.concatenate([share.reshape(64, 128), jnp.zeros((64, 128), F32)], axis=0)
        wt[p] = jnp.transpose(share)
        own_share = wt[p, pl.ds(pl.multiple_of(lax.rem(z, 8) * ROWS, ROWS), ROWS), :]
        lower = lax.broadcasted_iota(jnp.int32, (ROWS, 128), 1) < 64
        halves = [jnp.zeros((ROWS, 128), F32), jnp.zeros((ROWS, 128), F32)]
        for i in range(NZ):
            for n in range(2):
                low = jnp.broadcast_to(own_share[:, 4 * i + 2 * n : 4 * i + 2 * n + 1], (ROWS, 128))
                high = jnp.broadcast_to(own_share[:, 4 * i + 2 * n + 1 : 4 * i + 2 * n + 2], (ROWS, 128))
                halves[n] += jnp.where(lower, low, high) * rz[p, i, :, 128 * n : 128 * n + 128].astype(F32)
        att[p, y] = jnp.concatenate(halves, axis=1).astype(BF)
        for k in range(1, NY):
            put(att.at[p, y], att.at[p, y], base + GAY, dev_y(k)[1]).start()
        arrived(att.at[p, pl.ds(0, 3)], base + GAY)

        w_o = jnp.concatenate([ow[i, j].reshape(256, 128) for i in range(4) for j in range(2)], axis=1)
        ob[p, y] = dot_nt(jnp.concatenate([att[p, i] for i in range(NY)], axis=1), w_o)
        for k in range(1, NY):
            put(ob.at[p, y], ob.at[p, y], base + GOY, dev_y(k)[1]).start()
        if p == 0:
            arrived(up.at[pl.ds(0, 3), 0], UX)
            put(up.at[:, c], up.at[:, c], UC, partner).start()
        arrived(ob.at[p, pl.ds(0, 3)], base + GOY)
        residual = current.astype(F32) + jnp.concatenate([ob[p, i] for i in range(NY)], axis=1)
        settled = layer_norm(residual, ga_ref[...]).astype(BF)

        if p == 0:
            arrived(up.at[:, 0], UC)
        w_u = jnp.concatenate([up[i, j].reshape(D, 128) for i in range(4) for j in range(2)], axis=1)
        product = dot_nt(settled, w_u)
        hidden = (0.5 * product * (1.0 + lax.erf(product * (0.5**0.5)))).astype(BF)
        if p == 0:
            arrived(down.at[pl.ds(0, 3), 0], DX)
            put(down.at[:, c], down.at[:, c], DC, partner).start()
            arrived(down.at[:, 0], DC)
        w_d = jnp.concatenate([down[i, j].reshape(D, 128) for i in range(4) for j in range(2)], axis=1)
        fp[p, y] = dot_nn(hidden, w_d).astype(BF)
        for k in range(1, NY):
            put(fp.at[p, y], fp.at[p, y], base + RFY, dev_y(k)[1]).start()
        if p == 0:
            arrived(qw.at[:, 0], QC)
        arrived(fp.at[p, pl.ds(0, 3)], base + RFY)
        projected = fp[p, 0].astype(F32) + fp[p, 1].astype(F32) + fp[p, 2].astype(F32) + fp[p, 3].astype(F32)
        finished = layer_norm(settled.astype(F32) + projected, gm_ref[...])
        taken = accept_ref[p, :, 0:1] == 1
        current = jnp.where(taken, finished, current.astype(F32)).astype(BF)

    fin[...] = current
    quarter = pl.ds(pl.multiple_of(y * 256, 256), 256)
    fz[z] = fin[:, quarter]

    @pl.loop(1, NZ)
    def _(k):
        put(fz.at[z], fz.at[z], FIN_Z, dev_z(k)[1]).start()

    arrived(fz.at[pl.ds(0, NZ - 1)], FIN_Z)
    for k in range(1, NY):
        put(fz, out_ref.at[:, :, quarter], FIN_Y, dev_y(k)[1]).start()
    out_ref[:, :, quarter] = fz[...]
    arrived(out_ref.at[:, :, pl.ds(0, 768)], FIN_Y)

    sent(ws.at[pl.ds(0, 7)], WS)
    sent(up.at[0, 0, pl.ds(0, NZ - 1)], AZ)
    sent(kvw.at[0, 0, :, :, pl.ds(0, 3)], KVY)
    sent(ow.at[0, 0, :, :, pl.ds(0, 3)], OY)
    for ref, xs, cs in ((qw, QX, QC), (kvw, KVX, KVC), (ow, OX, OC), (up, UX, UC), (down, DX, DC)):
        sent(ref.at[pl.ds(0, 3), 0], xs)
        sent(ref.at[:, 0], cs)
    sent(up.at[0, 0, pl.ds(0, NZ - 1)], UZ)
    sent(down.at[0, 0, pl.ds(0, NZ - 1)], DZ)
    for p in range(2):
        base = 16 + 9 * p
        sent(qt.at[p, pl.ds(0, NZ - 1), 0], base + GQZ)
        sent(qt.at[p, :, pl.ds(0, 3)], base + GQY)
        sent(ry.at[p, pl.ds(0, 3)], base + RSY)
        sent(rym.at[p, pl.ds(0, 3)], base + RSYM)
        sent(rz.at[p, pl.ds(0, NZ - 1)], base + RSZ)
        sent(rzm.at[p, pl.ds(0, NZ - 1)], base + RSZM)
        sent(att.at[p, pl.ds(0, 3)], base + GAY)
        sent(ob.at[p, pl.ds(0, 3)], base + GOY)
        sent(fp.at[p, pl.ds(0, 3)], base + RFY)
    sent(fz.at[pl.ds(0, NZ - 1)], FIN_Z)
    sent(out_ref.at[:, :, pl.ds(0, 768)], FIN_Y)


def shards(
    block_in, accept, cache_len, slot_page, cache_kv, w_query, w_key_value, w_out, gain_attn, w_up, w_down, gain_mlp
):
    z = lax.div(lax.axis_index("tok"), NY)
    taken = lax.dynamic_slice_in_dim(accept[:, 0], z * ROWS, ROWS, 1)
    taken = jnp.broadcast_to(taken[:, :, None], (2, ROWS, 128))
    vmem = pl.BlockSpec(memory_space=pltpu.VMEM)
    smem = pl.BlockSpec(memory_space=pltpu.SMEM)
    result = pl.pallas_call(
        kernel,
        out_shape=jax.ShapeDtypeStruct((NZ, ROWS, D), BF),
        in_specs=[vmem, vmem, smem, smem, pl.BlockSpec(memory_space=pl.ANY)] + [vmem] * 7,
        out_specs=vmem,
        scratch_shapes=[
            pltpu.VMEM((3, 128, 2 * D), BF),
            pltpu.VMEM((8, 144, KEYS), BF),
            pltpu.VMEM((8, 16, 128), BF),
            pltpu.VMEM((2, 4, 2, 64, 128), BF),
            pltpu.VMEM((4, 2, 2, 4, 2, 16, 128), BF),
            pltpu.VMEM((4, 2, 2, 2, 4, 32, 128), BF),
            pltpu.VMEM((4, 2, 2, 2, 4, 16, 128), BF),
            pltpu.VMEM((4, 2, NZ, 64, 128), BF),
            pltpu.VMEM((4, 2, NZ, 64, 128), BF),
            pltpu.VMEM((ROWS, 256), BF),
            pltpu.VMEM((NZ, ROWS, 256), BF),
            pltpu.VMEM((2, NZ, NY, 16, TOK), BF),
            pltpu.VMEM((2, NY, 256, TOK), BF),
            pltpu.VMEM((2, NY, 8, TOK), F32),
            pltpu.VMEM((2, NY, 256, TOK), BF),
            pltpu.VMEM((2, NY, 8, TOK), F32),
            pltpu.VMEM((2, NZ, ROWS, 256), BF),
            pltpu.VMEM((2, 8, TOK), F32),
            pltpu.VMEM((2, NZ, ROWS, 256), BF),
            pltpu.VMEM((2, NZ, 8, 128), F32),
            pltpu.VMEM((2, 128, 128), F32),
            pltpu.VMEM((2, NY, ROWS, 256), BF),
            pltpu.VMEM((2, NY, ROWS, 256), F32),
            pltpu.VMEM((2, NY, ROWS, D), BF),
            pltpu.VMEM((ROWS, D), BF),
            pltpu.VMEM((NZ, ROWS, 256), BF),
            pltpu.SemaphoreType.DMA((N_SEM,)),
            pltpu.SemaphoreType.DMA((N_SEM,)),
            pltpu.SemaphoreType.DMA,
        ],
        compiler_params=pltpu.CompilerParams(
            collective_id=0, has_side_effects=True, vmem_limit_bytes=48 * 1024 * 1024
        ),
    )(
        block_in[0],
        taken,
        cache_len,
        slot_page,
        cache_kv[0],
        w_query.T,
        w_key_value.T,
        w_out.T,
        w_up.T,
        w_down,
        gain_attn[None],
        gain_mlp[None],
    )
    return result.reshape(1, TOK, D)


def solution(mesh):
    in_specs = (
        P("seq", None, None),
        P(None, "seq", None),
        P("seq"),
        P("seq", "tok"),
        P("seq", "tok", None, None),
        P("seq", "tok"),
        P("seq", "tok"),
        P("seq", "tok"),
        P(),
        P("seq", "tok"),
        P("tok", "seq"),
        P(),
    )
    out_specs = P("seq", None, None)
    return jax.shard_map(shards, mesh=mesh, in_specs=in_specs, out_specs=out_specs, check_vma=False)
```

time: 1600 us -> 170 us (0.11)
  the two profiles are of different devices: /device:TPU:2 before, /device:TPU:32 now
where the time goes in v1:
time: 170 us
  Pallas kernels  160 us (94%)
  local copies, waits for them, and re-layouts  8.94 us (5%)
    pallas_call x1, Pallas kernels, shards(): pl.pallas_call(kernel, out_shape=jax.ShapeDtypeStruct((NZ, ROWS, D), BF),...  160 us
    unnamed x23, local copies, waits for them, and re-layouts  8.79 us

profile of v1, /device:TPU:32, one launch (start us, length us, event | category | flops | bytes accessed | tf_op | source)
XLA Modules:
  0.0 169.7 jit_solution(10699448203258928303)
XLA Ops:
  0.0 0.0 copy-start
  0.7 0.0 copy-done
  0.7 0.1 constant_dynamic-slice_fusion
  0.8 0.1 broadcast_in_dim.15.accept_ref
  0.8 0.0 copy-start.1
  0.8 1.4 copy-done.1
  2.2 0.0 copy-start.2
  2.2 1.0 copy-done.2
  3.3 0.0 copy-start.3
  3.3 0.7 copy-done.3
  4.0 0.0 copy-start.4
  4.0 0.7 copy-done.4
  4.7 0.0 copy-start.5
  4.7 0.7 copy-done.5
  5.4 0.0 copy-start.6
  5.4 0.7 copy-done.6
  6.1 0.0 copy-start.7
  6.1 0.7 copy-done.7
  6.8 0.0 copy-start.8
  6.8 0.7 copy-done.8
  7.5 0.0 copy-start.9
  7.5 0.7 copy-done.9
  8.2 0.0 copy-start.10
  8.2 0.7 copy-done.10
  8.8 160.0 %shard_map.118 = bf16[16,16,1024]{2,1,0:T(8,128)(2,1)S(1)} custom-call(bf16[256,1024]{1,0:T(8,128)(2,1)S(1)} %bitcast.12, s32[2,16,128]{2,1,0:T(8,128)S(1)} %broadcast_in_dim.15.accept_ref, s32[1]{0:T(128)S(6)} %copy.14.len_ref, s32[1,3]{1,0:T(1,128)S(1)} %copy-done.10, bf16[3,128,2048]{2,1,0:T(8,128)(2,1)S(1)} %bitcast.11, bf16[16,128]{1,0:T(8,128)(2,1)S(1)} %bitcast.15, ...), custom_call_target="tpu_custom_call" | custom-call | tf_op jit(solution)/shard_map/pallas_call | solution.py:380
  168.9 0.8 copy.15
Async XLA Ops:
  0.0 0.7 copy-start
  0.8 1.4 copy-start.1
  2.2 1.0 copy-start.2
  3.3 0.7 copy-start.3
  4.0 0.7 copy-start.4
  4.7 0.7 copy-start.5
  5.4 0.7 copy-start.6
  6.1 0.7 copy-start.7
  6.8 0.7 copy-start.8
  7.5 0.7 copy-start.9
  8.2 0.7 copy-start.10

commit v2 on v1

v2 whole, which is shorter than its diff:
```python
import jax
import jax.numpy as jnp
from jax import lax
from jax.experimental import pallas as pl
from jax.experimental.pallas import tpu as pltpu
from jax.sharding import PartitionSpec as P

MESH = pl.DeviceIdType.MESH
BF = jnp.bfloat16
F32 = jnp.float32

D = 1024
TOK = 256
NZ, NY, NX = 16, 4, 4
ROWS = TOK // NZ
KEYS = 384
EPSILON = 1e-05
FLOOR_SCORE = -1e30
MASKED = -3e38

(WS, KVZ, OZ, QZ, KVX, OX, QX, KVC, OC, QC, UX, DX, UC, DC, LIM) = range(15)
CY = 15
UP, DOWN = 19, 23
PASS = 27
(GQZ, RSZ, RSZM, GAY, GOY, RFY) = range(6)
FIN_Y, FIN_Z = PASS + 12, PASS + 12
N_SEM = PASS + 28


def dot_nn(a, b):
    return lax.dot_general(a, b, (((1,), (0,)), ((), ())), preferred_element_type=F32)


def dot_nt(a, b):
    return lax.dot_general(a, b, (((1,), (1,)), ((), ())), preferred_element_type=F32)


def layer_norm(values, gain):
    average = jnp.mean(values, axis=-1, keepdims=True)
    centered = values - average
    variance = jnp.mean(centered * centered, axis=-1, keepdims=True)
    return centered * lax.rsqrt(variance + EPSILON) * gain


def kernel(
    len_ref, page_ref, x_hbm, accept_hbm, cache_ref, wq_ref, wkv_ref, wo_ref, wu_ref, wd_ref, ga_hbm, gm_hbm,
    out_ref,
    x_ref, accept_ref, ga_ref, gm_ref, kvb, vt, lim, ws, qw, kvw, ow, up, down,
    hold, qz, qt, po, pm, tz, tzm, rz, rzm, att, ob, fp, fin, fz,
    ssem, rsem, lsem,
):
    s, t = lax.axis_index("seq"), lax.axis_index("tok")
    x, c = lax.div(s, 2), lax.rem(s, 2)
    z, y = lax.div(t, NY), lax.rem(t, NY)
    za, zc = lax.div(z, 8), lax.rem(z, 2)
    to_kv = lax.div(lax.rem(z, 8), 2)
    to_q = lax.div(z, 4)
    to_t = lax.rem(t, NZ) * NY + lax.div(t, NZ)
    from_t = (NY * y + lax.div(z, NY)) * NY + lax.rem(z, NY)

    def dev_z(k, row=None):
        zp = lax.rem(z + k, NZ)
        return zp, {"seq": s, "tok": zp * NY + (y if row is None else row)}

    def dev_y(k):
        yp = lax.rem(y + k, NY)
        return yp, {"seq": s, "tok": z * NY + yp}

    def dev_s(k, tok):
        return {"seq": lax.rem(s + k, 2 * NX), "tok": tok}

    def dev_x(k):
        return {"seq": lax.rem(x + k, NX) * 2 + c, "tok": t}

    partner = {"seq": x * 2 + 1 - c, "tok": t}

    def put(src, dst, ph, dev, rph=None):
        return pltpu.make_async_remote_copy(
            src_ref=src,
            dst_ref=dst,
            send_sem=ssem.at[ph],
            recv_sem=rsem.at[ph if rph is None else rph],
            device_id=dev,
            device_id_type=MESH,
        )

    def arrived(view, ph):
        put(view, view, ph, partner).wait_recv()

    def sent(view, ph):
        put(view, view, ph, partner).wait_send()

    def here(src, dst, ph):
        pltpu.make_async_copy(src, dst, rsem.at[ph]).start()

    def tell(dev):
        pl.semaphore_signal(barrier, inc=1, device_id=dev, device_id_type=MESH)

    def lanes(start, size):
        return pl.ds(pl.multiple_of(start, size), size)

    local = [
        pltpu.make_async_copy(a, b, lsem.at[i])
        for i, (a, b) in enumerate(
            (
                (x_hbm, x_ref),
                (cache_ref.at[:, :, lanes(y * 256, 256)], kvb.at[y, 0]),
                (cache_ref.at[:, :, lanes(D + y * 256, 256)], kvb.at[y, 1]),
                (wu_ref, up.at[x, c, z]),
                (wd_ref, down.at[x, c, z]),
                (accept_hbm, accept_ref),
                (ga_hbm, ga_ref),
                (gm_hbm, gm_ref),
            )
        )
    ]
    for copy in local:
        copy.start()

    barrier = pltpu.get_barrier_semaphore()
    for k in range(8):
        @pl.when((k > 0) | (from_t != t))
        def _():
            tell(dev_s(k, from_t))
    for k in range(1, NX):
        tell(dev_x(k))
    tell(partner)
    for k in range(1, NY):
        tell(dev_y(k)[1])

    @pl.loop(1, NZ)
    def _(k):
        tell(dev_z(k)[1])

    @pl.loop(0, NZ)
    def _(i):
        zs, ys = 8 * lax.div(i, 8) + 2 * y + lax.rem(lax.div(i, 4), 2), lax.rem(i, 4)

        @pl.when((zs != z) | (ys != y))
        def _():
            tell({"seq": s, "tok": zs * NY + ys})

    @pl.loop(0, NZ)
    def _(i):
        zs, ys = 4 * y + lax.div(i, 4), lax.rem(i, 4)

        @pl.when((zs != z) | (ys != y))
        def _():
            tell({"seq": s, "tok": zs * NY + ys})

    others = (to_t != t).astype(jnp.int32) + (to_kv != y).astype(jnp.int32) + (to_q != y).astype(jnp.int32)
    pl.semaphore_wait(barrier, 7 + NX + (NY - 1) + 3 * (NZ - 1) + others)

    for k in range(8):
        @pl.when((k > 0) | (to_t != t))
        def _():
            put(wq_ref, ws.at[s], WS, dev_s(k, to_t)).start()

    @pl.when(to_t == t)
    def _():
        here(wq_ref, ws.at[s], WS)

    for k in (1, 3, 2):
        yp, dev = dev_y(k)
        put(cache_ref.at[:, :, lanes(yp * 256, 256)], kvb.at[y, 0], CY + k, dev).start()
        put(cache_ref.at[:, :, lanes(D + yp * 256, 256)], kvb.at[y, 1], CY + k, dev).start()
    length = len_ref[0].astype(F32)
    slot_row = lax.broadcasted_iota(jnp.int32, (8, 128), 0)
    limits = jnp.zeros((8, 128), F32)
    for j in range(3):
        page = page_ref[0, j].astype(F32)
        limits = jnp.where(slot_row == j, jnp.where(page >= 0, length - page * 128, 0.0), limits)
    lim[y] = limits
    for k in range(1, NY):
        put(lim.at[y], lim.at[y], LIM, dev_y(k)[1]).start()

    def spread(src, dst, ph, row):
        @pl.loop(1, NZ)
        def _(k):
            put(src, dst, ph, dev_z(k, row)[1]).start()

        @pl.when(row != y)
        def _():
            put(src, dst, ph, dev_z(0, row)[1]).start()

        @pl.when(row == y)
        def _():
            here(src, dst, ph)

    spread(wkv_ref, kvw.at[x, c, za, zc, y], KVZ, to_kv)
    arrived(ws, WS)
    local[0].wait()
    wq_cols = jnp.concatenate([ws[i] for i in range(8)], axis=1)
    qt[0, z] = dot_nt(wq_cols, x_ref[...]).astype(BF) * jnp.asarray(0.125, BF)

    @pl.loop(1, NZ)
    def _(k):
        put(qt.at[0, z], qt.at[0, z], PASS + GQZ, dev_z(k)[1]).start()

    def direct(ref, ph):
        for k in (4, 12):
            put(ref.at[x, c, z], ref.at[x, c, z], ph, dev_z(k)[1], ph + (1 if k == 4 else 2)).start()
        for k in (1, 15, 2, 14, 3, 13):
            put(ref.at[x, c, z], ref.at[x, c, z], ph, dev_z(k)[1]).start()

    def relay(ref, ph):
        left, right = lax.rem(z + 12, NZ), lax.rem(z + 4, NZ)
        arrived(ref.at[x, c, left], ph + 1)
        for k in (4, 3, 2, 1):
            put(ref.at[x, c, left], ref.at[x, c, left], ph + 3, dev_z(k)[1]).start()
        arrived(ref.at[x, c, right], ph + 2)
        for k in (13, 14, 15):
            put(ref.at[x, c, right], ref.at[x, c, right], ph + 3, dev_z(k)[1]).start()

    def to_x(ref, ph):
        for k in (1, 3, 2):
            put(ref.at[x, c], ref.at[x, c], ph, dev_x(k)).start()

    def to_core(ref, xs, cs):
        arrived(ref.at[pl.ds(0, 3), 0], xs)
        put(ref.at[:, c], ref.at[:, c], cs, partner).start()

    def over_z(ref, ph, xs):
        arrived(ref.at[0, 0, pl.ds(0, 6)], ph)
        arrived(ref.at[0, 0, pl.ds(0, 7)], ph + 3)
        to_x(ref, xs)

    spread(wo_ref, ow.at[x, c, lax.rem(z, 4), y], OZ, to_q)
    local[3].wait()
    direct(up, UP)
    local[4].wait()
    direct(down, DOWN)
    spread(wq_ref, qw.at[x, c, lax.rem(z, 4), y], QZ, to_q)

    vt[:, :, 128:144, :] = jnp.ones((NY, 2, 16, KEYS), BF)

    def turn(j):
        for i in range(2):
            for n in range(3):
                vt[j, i, 0:128, 128 * n : 128 * (n + 1)] = jnp.transpose(kvb[j, 1, n, :, 128 * i : 128 * i + 128])

    local[1].wait()
    local[2].wait()
    turn(y)
    arrived(kvw.at[0, 0], KVZ)
    to_x(kvw, KVX)
    for k in (1, 3, 2):
        src = lax.rem(y + NY - k, NY)
        arrived(kvb.at[src], CY + k)
        turn(src)
    arrived(lim.at[pl.ds(0, 3)], LIM)
    for i in range(5, 8):
        local[i].wait()

    own_rows = pl.ds(pl.multiple_of(z * ROWS, ROWS), ROWS)
    current = x_ref[own_rows, :]

    for p in range(2):
        base = PASS + 6 * p
        if p == 1:
            w_q = jnp.concatenate([qw[i, j].reshape(256, 128) for i in range(4) for j in range(2)], axis=1)
            qz[z] = dot_nt(current, w_q).astype(BF) * jnp.asarray(0.125, BF)

            @pl.loop(1, NZ)
            def _(k):
                put(qz.at[z], qz.at[z], base + GQZ, dev_z(k)[1]).start()

            arrived(qz.at[pl.ds(0, NZ - 1)], base + GQZ)
            qt[1] = jnp.transpose(qz[...].reshape(TOK, 256)).reshape(NZ, 16, TOK)
        else:
            arrived(qt.at[p, pl.ds(0, NZ - 1)], base + GQZ)

        @pl.loop(0, NY)
        def _(j):
            if p == 0:
                @pl.when(j == 1)
                def _():
                    arrived(ow.at[0, 0], OZ)
                    to_x(ow, OX)
                    to_core(kvw, KVX, KVC)

                @pl.when(j == 2)
                def _():
                    relay(up, UP)

                @pl.when(j == 3)
                def _():
                    relay(down, DOWN)

            for i in range(2):
                keys = kvb[j, 0, :, :, 128 * i : 128 * i + 128].reshape(KEYS, 128)
                q_pair = qt[p, 8 * i : 8 * i + 8].reshape(2, 64, TOK)
                none = jnp.zeros((64, TOK), BF)
                both = jnp.concatenate(
                    [
                        jnp.concatenate([q_pair[0], none], axis=1),
                        jnp.concatenate([none, q_pair[1]], axis=1),
                    ],
                    axis=0,
                )
                scores = dot_nn(keys, both)
                offsets = lax.broadcasted_iota(jnp.int32, (128, 2 * TOK), 0).astype(F32)
                masked = jnp.concatenate(
                    [
                        jnp.where(
                            offsets < jnp.concatenate([lim[j, n : n + 1, :]] * 4, axis=1),
                            scores[128 * n : 128 * (n + 1)],
                            MASKED,
                        )
                        for n in range(3)
                    ],
                    axis=0,
                )
                peaks = jnp.maximum(jnp.max(masked, axis=0, keepdims=True), FLOOR_SCORE)
                weights = jnp.exp(masked - peaks).astype(BF)
                summed = dot_nn(vt[j, i], weights)
                po[j, 128 * i : 128 * i + 64, :] = summed[0:64, 0:TOK]
                po[j, 128 * i + 64 : 128 * i + 128, :] = summed[64:128, TOK : 2 * TOK]
                pm[j, 2 * i : 2 * i + 1, :] = peaks[:, 0:TOK]
                pm[j, 2 * i + 1 : 2 * i + 2, :] = peaks[:, TOK : 2 * TOK]
                pm[j, 4 + 2 * i : 5 + 2 * i, :] = summed[128:129, 0:TOK]
                pm[j, 5 + 2 * i : 6 + 2 * i, :] = summed[128:129, TOK : 2 * TOK]

        if p == 0:
            over_z(up, UP, UX)
            arrived(kvw.at[:, 0], KVC)

        w_pair = jnp.concatenate([kvw[i, j].reshape(512, 128) for i in range(4) for j in range(2)], axis=1)
        pair = dot_nt(current, w_pair)
        row_head = lax.div(lax.broadcasted_iota(jnp.int32, (64, 256), 0), 16)
        lane_head = lax.div(lax.broadcasted_iota(jnp.int32, (64, 256), 1), 64)
        own_head = row_head == lane_head
        k_block = jnp.where(own_head, jnp.concatenate([pair[:, 0:256]] * 4, axis=0), 0.0).astype(BF)
        v_block = jnp.where(own_head, jnp.concatenate([pair[:, 256:512]] * 4, axis=0), 0.0)
        b_scores = dot_nn(k_block, qt[p].reshape(256, TOK)).reshape(4, 16, TOK)
        b_peak = jnp.max(b_scores, axis=1)
        b_weights = jnp.exp(b_scores - b_peak[:, None, :]).astype(BF)
        b_total = jnp.sum(b_weights.astype(F32), axis=1)
        b_sum = dot_nn(jnp.transpose(v_block).astype(BF), b_weights.reshape(64, TOK))

        peaks_y = pm[:, 0:4, :]
        peak = jnp.maximum(jnp.max(peaks_y, axis=0), b_peak)
        scale = jnp.exp(peaks_y - peak[None])
        b_scale = jnp.exp(b_peak - peak)
        total = jnp.sum(scale * pm[:, 4:8, :], axis=0) + b_scale * b_total
        parts = []
        for h in range(4):
            rows = slice(64 * h, 64 * h + 64)
            value = b_sum[rows] * b_scale[h : h + 1]
            for i in range(NY):
                value += po[i, rows, :] * scale[i, h : h + 1]
            parts.append(value)
        tz[p] = jnp.transpose(jnp.concatenate(parts, axis=0)).astype(BF).reshape(NZ, ROWS, 256)
        both = jnp.concatenate([peak, total], axis=0)
        belongs = lax.broadcasted_iota(jnp.int32, (8, 128), 0) == lax.div(
            lax.broadcasted_iota(jnp.int32, (8, 128), 1), ROWS
        )
        steps = [pltpu.roll(both[:, 128 * i : 128 * i + 128], 0, 1, stride=ROWS, stride_axis=0) for i in range(2)]
        for i in range(NZ):
            moved = pltpu.roll(steps[i // 8], (128 - ROWS * (i % 8)) % 128, 1)
            tzm[p, i] = jnp.sum(jnp.where(belongs, moved, 0.0), axis=0, keepdims=True)

        @pl.loop(1, NZ)
        def _(k):
            zp, dev = dev_z(k)
            put(tzm.at[p, zp], rzm.at[p, z], base + RSZM, dev).start()
            put(tz.at[p, zp], rz.at[p, z], base + RSZ, dev).start()

        rz[p, z] = tz[p, z]
        rzm[p, z] = tzm[p, z]
        if p == 0:
            over_z(down, DOWN, DX)
            to_core(ow, OX, OC)

        arrived(rzm.at[p, pl.ds(0, NZ - 1)], base + RSZM)
        stats = rzm[p].reshape(NZ, 128)
        scale_z = jnp.exp(stats - jnp.max(stats, axis=0, keepdims=True))
        share = scale_z / jnp.sum(scale_z * pltpu.roll(stats, 64, 1), axis=0, keepdims=True)
        share = jnp.transpose(jnp.concatenate([share, jnp.zeros((128 - NZ, 128), F32)], axis=0))
        arrived(rz.at[p, pl.ds(0, NZ - 1)], base + RSZ)
        lower = lax.broadcasted_iota(jnp.int32, (ROWS, 128), 1) < 64
        halves = [jnp.zeros((ROWS, 128), F32), jnp.zeros((ROWS, 128), F32)]
        for i in range(NZ):
            for n in range(2):
                low = jnp.broadcast_to(share[32 * n : 32 * n + 16, i : i + 1], (ROWS, 128))
                high = jnp.broadcast_to(share[32 * n + 16 : 32 * n + 32, i : i + 1], (ROWS, 128))
                halves[n] += jnp.where(lower, low, high) * rz[p, i, :, 128 * n : 128 * n + 128].astype(F32)
        att[p, y] = jnp.concatenate(halves, axis=1).astype(BF)
        for k in range(1, NY):
            put(att.at[p, y], att.at[p, y], base + GAY, dev_y(k)[1]).start()
        if p == 0:
            arrived(ow.at[:, 0], OC)
            arrived(qw.at[0, 0], QZ)
            to_x(qw, QX)
        arrived(att.at[p, pl.ds(0, 3)], base + GAY)

        w_o = jnp.concatenate([ow[i, j].reshape(256, 128) for i in range(4) for j in range(2)], axis=1)
        ob[p, y] = dot_nt(jnp.concatenate([att[p, i] for i in range(NY)], axis=1), w_o)
        for k in range(1, NY):
            put(ob.at[p, y], ob.at[p, y], base + GOY, dev_y(k)[1]).start()
        if p == 0:
            to_core(up, UX, UC)
        arrived(ob.at[p, pl.ds(0, 3)], base + GOY)
        residual = current.astype(F32) + jnp.concatenate([ob[p, i] for i in range(NY)], axis=1)
        settled = layer_norm(residual, ga_ref[...]).astype(BF)

        if p == 0:
            arrived(up.at[:, 0], UC)
        w_u = jnp.concatenate([up[i, j].reshape(D, 128) for i in range(4) for j in range(2)], axis=1)
        product = dot_nt(settled, w_u)
        hidden = (0.5 * product * (1.0 + lax.erf(product * (0.5**0.5)))).astype(BF)
        if p == 0:
            to_core(down, DX, DC)
            arrived(down.at[:, 0], DC)
        w_d = jnp.concatenate([down[i, j].reshape(D, 128) for i in range(4) for j in range(2)], axis=1)
        fp[p, y] = dot_nn(hidden, w_d).astype(BF)
        for k in range(1, NY):
            put(fp.at[p, y], fp.at[p, y], base + RFY, dev_y(k)[1]).start()
        if p == 0:
            to_core(qw, QX, QC)
            arrived(qw.at[:, 0], QC)
        arrived(fp.at[p, pl.ds(0, 3)], base + RFY)
        projected = fp[p, 0].astype(F32) + fp[p, 1].astype(F32) + fp[p, 2].astype(F32) + fp[p, 3].astype(F32)
        finished = layer_norm(settled.astype(F32) + projected, gm_ref[...])
        own_token = lax.broadcasted_iota(jnp.int32, (ROWS, TOK), 1) == z * ROWS + lax.broadcasted_iota(
            jnp.int32, (ROWS, TOK), 0
        )
        taken = jnp.sum(jnp.where(own_token, accept_ref[p].astype(F32), 0.0), axis=1, keepdims=True) > 0.5
        current = jnp.where(taken, finished, current.astype(F32)).astype(BF)

    fin[...] = current
    quarter = lanes(y * 256, 256)
    fz[z] = fin[:, quarter]

    def hand_on(zp):
        for k in range(1, NY):
            put(fz.at[zp], out_ref.at[zp, :, quarter], FIN_Y, dev_y(k)[1]).start()

    def in_turn(i):
        near = lax.div(i, 2) + 1
        return jnp.where(lax.rem(i, 2) == 0, near, NZ - near)

    @pl.loop(0, NZ - 1)
    def _(i):
        k = in_turn(i)
        put(fz.at[z], fz.at[z], FIN_Z + k, dev_z(k)[1]).start()

    hand_on(z)

    @pl.loop(0, NZ - 1)
    def _(i):
        k = in_turn(i)
        zp = lax.rem(z + NZ - k, NZ)
        arrived(fz.at[zp], FIN_Z + k)
        hand_on(zp)

    out_ref[:, :, quarter] = fz[...]
    arrived(out_ref.at[:, :, pl.ds(0, 768)], FIN_Y)

    def sent_but_own(ref, axis_end, ph, own):
        @pl.when(own)
        def _():
            sent(ref.at[pl.ds(0, axis_end - 1)], ph)

        @pl.when(jnp.logical_not(own))
        def _():
            sent(ref.at[pl.ds(0, axis_end)], ph)

    sent_but_own(ws, 8, WS, to_t == t)
    sent_but_own(qz, NZ, KVZ, to_kv == y)
    sent_but_own(hold, NZ, OZ, to_q == y)
    sent_but_own(hold, NZ, QZ, to_q == y)
    for ref, xs, cs in ((qw, QX, QC), (kvw, KVX, KVC), (ow, OX, OC), (up, UX, UC), (down, DX, DC)):
        sent(ref.at[pl.ds(0, 3), 0], xs)
        sent(ref.at[:, 0], cs)
    for ph in (UP, DOWN):
        sent(up.at[0, 0, pl.ds(0, 8)], ph)
        sent(up.at[0, 0, pl.ds(0, 7)], ph + 3)
    for k in range(1, NY):
        sent(kvb.at[0], CY + k)
    sent(lim.at[pl.ds(0, 3)], LIM)
    for p in range(2):
        base = PASS + 6 * p
        sent(qz.at[pl.ds(0, NZ - 1)], base + GQZ)
        sent(rz.at[p, pl.ds(0, NZ - 1)], base + RSZ)
        sent(rzm.at[p, pl.ds(0, NZ - 1)], base + RSZM)
        sent(att.at[p, pl.ds(0, 3)], base + GAY)
        sent(ob.at[p, pl.ds(0, 3)], base + GOY)
        sent(fp.at[p, pl.ds(0, 3)], base + RFY)

    @pl.loop(1, NZ)
    def _(k):
        sent(fz.at[0], FIN_Z + k)

    sent(out_ref.at[:, :, pl.ds(0, 768)], FIN_Y)


def shards(
    block_in, accept, cache_len, slot_page, cache_kv, w_query, w_key_value, w_out, gain_attn, w_up, w_down, gain_mlp
):
    smem = pl.BlockSpec(memory_space=pltpu.SMEM)
    result = pl.pallas_call(
        kernel,
        out_shape=jax.ShapeDtypeStruct((NZ, ROWS, D), BF),
        in_specs=[smem, smem] + [pl.BlockSpec(memory_space=pl.ANY)] * 10,
        out_specs=pl.BlockSpec(memory_space=pltpu.VMEM),
        scratch_shapes=[
            pltpu.VMEM((TOK, D), BF),
            pltpu.VMEM((2, 1, TOK), jnp.int32),
            pltpu.VMEM((1, D), F32),
            pltpu.VMEM((1, D), F32),
            pltpu.VMEM((NY, 2, 3, 128, 256), BF),
            pltpu.VMEM((NY, 2, 144, KEYS), BF),
            pltpu.VMEM((NY, 8, 128), F32),
            pltpu.VMEM((8, 16, 128), BF),
            pltpu.VMEM((4, 2, 4, 4, 16, 128), BF),
            pltpu.VMEM((4, 2, 2, 2, 4, 32, 128), BF),
            pltpu.VMEM((4, 2, 4, 4, 16, 128), BF),
            pltpu.VMEM((4, 2, NZ, 64, 128), BF),
            pltpu.VMEM((4, 2, NZ, 64, 128), BF),
            pltpu.VMEM((NZ, 16, 128), BF),
            pltpu.VMEM((NZ, ROWS, 256), BF),
            pltpu.VMEM((2, NZ, 16, TOK), BF),
            pltpu.VMEM((NY, 256, TOK), F32),
            pltpu.VMEM((NY, 8, TOK), F32),
            pltpu.VMEM((2, NZ, ROWS, 256), BF),
            pltpu.VMEM((2, NZ, 1, 128), F32),
            pltpu.VMEM((2, NZ, ROWS, 256), BF),
            pltpu.VMEM((2, NZ, 1, 128), F32),
            pltpu.VMEM((2, NY, ROWS, 256), BF),
            pltpu.VMEM((2, NY, ROWS, 256), F32),
            pltpu.VMEM((2, NY, ROWS, D), BF),
            pltpu.VMEM((ROWS, D), BF),
            pltpu.VMEM((NZ, ROWS, 256), BF),
            pltpu.SemaphoreType.DMA((N_SEM,)),
            pltpu.SemaphoreType.DMA((N_SEM,)),
            pltpu.SemaphoreType.DMA((8,)),
        ],
        compiler_params=pltpu.CompilerParams(
            collective_id=0, has_side_effects=True, vmem_limit_bytes=48 * 1024 * 1024
        ),
    )(
        cache_len,
        slot_page,
        block_in[0],
        accept,
        cache_kv[0],
        w_query.T,
        w_key_value.T,
        w_out.T,
        w_up.T,
        w_down,
        gain_attn[None],
        gain_mlp[None],
    )
    return result.reshape(1, TOK, D)


def solution(mesh):
    in_specs = (
        P("seq", None, None),
        P(None, "seq", None),
        P("seq"),
        P("seq", "tok"),
        P("seq", "tok", None, None),
        P("seq", "tok"),
        P("seq", "tok"),
        P("seq", "tok"),
        P(),
        P("seq", "tok"),
        P("tok", "seq"),
        P(),
    )
    out_specs = P("seq", None, None)
    return jax.shard_map(shards, mesh=mesh, in_specs=in_specs, out_specs=out_specs, check_vma=False)
```

time: 170 us -> 152 us (0.89)
  Pallas kernels: 160 us -> 142 us
    pallas_call x1, Pallas kernels: 160 us -> 142 us  [shards(): pl.pallas_call(kernel, out_shape=jax.ShapeDtypeStruct((NZ, ROWS, D), BF),...]
where the time goes in v2:
time: 152 us
  Pallas kernels  142 us (93%)
  local copies, waits for them, and re-layouts  9.45 us (6%)
    pallas_call x1, Pallas kernels, shards(): pl.pallas_call(kernel, out_shape=jax.ShapeDtypeStruct((NZ, ROWS, D), BF),...  142 us
    unnamed x23, local copies, waits for them, and re-layouts  9.45 us

profile of v2, /device:TPU:32, one launch (start us, length us, event | category | flops | bytes accessed | tf_op | source)
XLA Modules:
  0.0 151.7 jit_solution(10117187910403739901)
XLA Ops:
  0.7 0.0 copy-start
  0.7 1.4 copy-done
  2.1 0.0 copy-start.1
  2.1 1.0 copy-done.1
  3.1 0.0 copy-start.2
  3.1 0.7 copy-done.2
  3.8 0.0 copy-start.3
  3.8 0.7 copy-done.3
  4.5 0.0 copy-start.4
  4.5 0.7 copy-done.4
  5.2 0.0 copy-start.5
  5.2 0.7 copy-done.5
  5.9 0.0 copy-start.6
  5.9 0.7 copy-done.6
  6.6 0.0 copy-start.7
  6.6 0.7 copy-done.7
  7.3 0.0 copy-start.8
  7.3 0.7 copy-done.8
  8.0 0.0 copy-start.9
  8.0 0.7 copy-done.9
  8.7 0.0 copy-start.10
  8.7 0.7 copy-done.10
  9.3 141.6 %shard_map.118 = bf16[16,16,1024]{2,1,0:T(8,128)(2,1)S(1)} custom-call(s32[1]{0:T(128)S(6)} %copy.14.len_ref, s32[1,3]{1,0:T(1,128)S(1)} %copy-done.10, bf16[256,1024]{1,0:T(8,128)(2,1)S(1)} %bitcast.11, s32[2,1,256]{2,1,0:T(1,128)S(1)} %copy-done.9, bf16[3,128,2048]{2,1,0:T(8,128)(2,1)S(1)} %bitcast.10, bf16[16,128]{1,0:T(8,128)(2,1)S(1)} %bitcast.14, ...), custom_call_target="tpu_custom_call" | custom-call | tf_op jit(solution)/shard_map/pallas_call | solution.py:502
  150.9 0.8 copy.15
Async XLA Ops:
  0.7 1.4 copy-start
  2.1 1.0 copy-start.1
  3.1 0.7 copy-start.2
  3.8 0.7 copy-start.3
  4.5 0.7 copy-start.4
  5.2 0.7 copy-start.5
  5.9 0.7 copy-start.6
  6.6 0.7 copy-start.7
  7.3 0.7 copy-start.8
  8.0 0.7 copy-start.9
  8.7 0.7 copy-start.10

commit v3 on v2

--- a/solution.py
+++ b/solution.py
@@ -18,10 +18,11 @@
 FLOOR_SCORE = -1e30
 MASKED = -3e38
 
-(WS, KVZ, OZ, QZ, KVX, OX, QX, KVC, OC, QC, UX, DX, UC, DC, LIM) = range(15)
-CY = 15
-UP, DOWN = 19, 23
-PASS = 27
+(WS, KVZ, OZ, QZ, KVX, OX, QX, KVC, OC, QC, WS2, KPZ, LIM) = range(13)
+CY = 13
+UP, DOWN = 17, 25
+PASS = 33
+FAR_FIRST = (8, 7, 9, 6, 10, 5, 11, 4, 12, 3, 13, 2, 14, 1, 15)
 (GQZ, RSZ, RSZM, GAY, GOY, RFY) = range(6)
 FIN_Y, FIN_Z = PASS + 12, PASS + 12
 N_SEM = PASS + 28
@@ -45,7 +46,7 @@
 def kernel(
     len_ref, page_ref, x_hbm, accept_hbm, cache_ref, wq_ref, wkv_ref, wo_ref, wu_ref, wd_ref, ga_hbm, gm_hbm,
     out_ref,
-    x_ref, accept_ref, ga_ref, gm_ref, kvb, vt, lim, ws, qw, kvw, ow, up, down,
+    x_ref, accept_ref, ga_ref, gm_ref, kvb, vt, lim, ws, ws2, kp, rkp, qw, kvw, ow, up, down,
     hold, qz, qt, po, pm, tz, tzm, rz, rzm, att, ob, fp, fin, fz,
     ssem, rsem, lsem,
 ):
@@ -57,6 +58,8 @@
     to_q = lax.div(z, 4)
     to_t = lax.rem(t, NZ) * NY + lax.div(t, NZ)
     from_t = (NY * y + lax.div(z, NY)) * NY + lax.rem(z, NY)
+    to_p = (lax.rem(t, 8) + 8 * lax.div(t, 32)) * NY + lax.rem(lax.div(t, 8), 4)
+    from_p = 8 * y + z + 24 * za
 
     def dev_z(k, row=None):
         zp = lax.rem(z + k, NZ)
@@ -122,6 +125,10 @@
         @pl.when((k > 0) | (from_t != t))
         def _():
             tell(dev_s(k, from_t))
+
+        @pl.when((k > 0) | (from_p != t))
+        def _():
+            tell(dev_s(k, from_p))
     for k in range(1, NX):
         tell(dev_x(k))
     tell(partner)
@@ -149,16 +156,25 @@
             tell({"seq": s, "tok": zs * NY + ys})
 
     others = (to_t != t).astype(jnp.int32) + (to_kv != y).astype(jnp.int32) + (to_q != y).astype(jnp.int32)
-    pl.semaphore_wait(barrier, 7 + NX + (NY - 1) + 3 * (NZ - 1) + others)
+    others += (to_p != t).astype(jnp.int32)
+    pl.semaphore_wait(barrier, 14 + NX + (NY - 1) + 3 * (NZ - 1) + others)
 
     for k in range(8):
         @pl.when((k > 0) | (to_t != t))
         def _():
             put(wq_ref, ws.at[s], WS, dev_s(k, to_t)).start()
+
+        @pl.when((k > 0) | (to_p != t))
+        def _():
+            put(wkv_ref, ws2.at[s], WS2, dev_s(k, to_p)).start()
 
     @pl.when(to_t == t)
     def _():
         here(wq_ref, ws.at[s], WS)
+
+    @pl.when(to_p == t)
+    def _():
+        here(wkv_ref, ws2.at[s], WS2)
 
     for k in (1, 3, 2):
         yp, dev = dev_y(k)
@@ -187,21 +203,10 @@
         def _():
             here(src, dst, ph)
 
-    spread(wkv_ref, kvw.at[x, c, za, zc, y], KVZ, to_kv)
-    arrived(ws, WS)
-    local[0].wait()
-    wq_cols = jnp.concatenate([ws[i] for i in range(8)], axis=1)
-    qt[0, z] = dot_nt(wq_cols, x_ref[...]).astype(BF) * jnp.asarray(0.125, BF)
-
-    @pl.loop(1, NZ)
-    def _(k):
-        put(qt.at[0, z], qt.at[0, z], PASS + GQZ, dev_z(k)[1]).start()
-
-    def direct(ref, ph):
-        for k in (4, 12):
-            put(ref.at[x, c, z], ref.at[x, c, z], ph, dev_z(k)[1], ph + (1 if k == 4 else 2)).start()
-        for k in (1, 15, 2, 14, 3, 13):
-            put(ref.at[x, c, z], ref.at[x, c, z], ph, dev_z(k)[1]).start()
+    def direct(src, ref, ph):
+        for k in (4, 12, 3, 13, 2, 14, 1, 15):
+            landed = ph + {4: 1, 12: 2}.get(k, 0)
+            put(src, ref.at[x, c, z], ph, dev_z(k)[1], landed).start()
 
     def relay(ref, ph):
         left, right = lax.rem(z + 12, NZ), lax.rem(z + 4, NZ)
@@ -212,25 +217,61 @@
         for k in (13, 14, 15):
             put(ref.at[x, c, right], ref.at[x, c, right], ph + 3, dev_z(k)[1]).start()
 
+    def part(n):
+        return (0, 9) if n == 0 else (9, 16)
+
     def to_x(ref, ph):
-        for k in (1, 3, 2):
+        for k in (2, 1, 3):
             put(ref.at[x, c], ref.at[x, c], ph, dev_x(k)).start()
+
+    def ff_to_x(ref, ph, n):
+        if n == 0:
+            arrived(ref.at[0, 0, pl.ds(0, 6)], ph)
+        else:
+            arrived(ref.at[0, 0, pl.ds(0, 7)], ph + 3)
+
+        @pl.loop(*part(n))
+        def _(i):
+            slot = lax.rem(z + 12 + i, NZ)
+            for k in (2, 1, 3):
+                put(ref.at[x, c, slot], ref.at[x, c, slot], ph + 4 + n, dev_x(k)).start()
+
+    def ff_to_core(ref, ph, n):
+        low, high = part(n)
+        arrived(ref.at[pl.ds(0, 3), 0, pl.ds(0, high - low)], ph + 4 + n)
+
+        @pl.loop(low, high)
+        def _(i):
+            slot = lax.rem(z + 12 + i, NZ)
+            put(ref.at[:, c, slot], ref.at[:, c, slot], ph + 6 + n, partner).start()
+
+    def ff_ready(ref, ph):
+        for n in range(2):
+            low, high = part(n)
+            arrived(ref.at[:, 0, pl.ds(0, high - low)], ph + 6 + n)
 
     def to_core(ref, xs, cs):
         arrived(ref.at[pl.ds(0, 3), 0], xs)
         put(ref.at[:, c], ref.at[:, c], cs, partner).start()
 
-    def over_z(ref, ph, xs):
-        arrived(ref.at[0, 0, pl.ds(0, 6)], ph)
-        arrived(ref.at[0, 0, pl.ds(0, 7)], ph + 3)
-        to_x(ref, xs)
-
+    direct(wu_ref, up, UP)
+    direct(wd_ref, down, DOWN)
+    arrived(ws, WS)
+    local[0].wait()
+    wq_cols = jnp.concatenate([ws[i] for i in range(8)], axis=1)
+    qt[0, z] = dot_nt(wq_cols, x_ref[...]).astype(BF) * jnp.asarray(0.125, BF)
+
+    for k in FAR_FIRST:
+        put(qt.at[0, z], qt.at[0, z], PASS + GQZ, dev_z(k)[1]).start()
+    arrived(ws2, WS2)
+    kv_cols = jnp.concatenate([ws2[i] for i in range(8)], axis=1)
+    kv_cols = jnp.concatenate([kv_cols, jnp.zeros((96, D), BF)], axis=0)
+    kp[...] = dot_nt(x_ref[...], kv_cols).astype(BF).reshape(NZ, ROWS, 128)
+    for k in FAR_FIRST:
+        zp, dev = dev_z(k)
+        put(kp.at[zp], rkp.at[z], KPZ, dev).start()
+    rkp[z] = kp[z]
     spread(wo_ref, ow.at[x, c, lax.rem(z, 4), y], OZ, to_q)
-    local[3].wait()
-    direct(up, UP)
-    local[4].wait()
-    direct(down, DOWN)
-    spread(wq_ref, qw.at[x, c, lax.rem(z, 4), y], QZ, to_q)
 
     vt[:, :, 128:144, :] = jnp.ones((NY, 2, 16, KEYS), BF)
 
@@ -242,8 +283,12 @@
     local[1].wait()
     local[2].wait()
     turn(y)
-    arrived(kvw.at[0, 0], KVZ)
-    to_x(kvw, KVX)
+    local[3].wait()
+    local[4].wait()
+    relay(up, UP)
+    ff_to_x(up, UP, 0)
+    relay(down, DOWN)
+    ff_to_x(down, DOWN, 0)
     for k in (1, 3, 2):
         src = lax.rem(y + NY - k, NY)
         arrived(kvb.at[src], CY + k)
@@ -261,10 +306,9 @@
             w_q = jnp.concatenate([qw[i, j].reshape(256, 128) for i in range(4) for j in range(2)], axis=1)
             qz[z] = dot_nt(current, w_q).astype(BF) * jnp.asarray(0.125, BF)
 
-            @pl.loop(1, NZ)
-            def _(k):
+            for k in FAR_FIRST:
                 put(qz.at[z], qz.at[z], base + GQZ, dev_z(k)[1]).start()
-
+            arrived(kvw.at[:, 0], KVC)
             arrived(qz.at[pl.ds(0, NZ - 1)], base + GQZ)
             qt[1] = jnp.transpose(qz[...].reshape(TOK, 256)).reshape(NZ, 16, TOK)
         else:
@@ -277,15 +321,10 @@
                 def _():
                     arrived(ow.at[0, 0], OZ)
                     to_x(ow, OX)
-                    to_core(kvw, KVX, KVC)
-
-                @pl.when(j == 2)
-                def _():
-                    relay(up, UP)
 
                 @pl.when(j == 3)
                 def _():
-                    relay(down, DOWN)
+                    ff_to_x(up, UP, 1)
 
             for i in range(2):
                 keys = kvb[j, 0, :, :, 128 * i : 128 * i + 128].reshape(KEYS, 128)
@@ -322,11 +361,16 @@
                 pm[j, 5 + 2 * i : 6 + 2 * i, :] = summed[128:129, TOK : 2 * TOK]
 
         if p == 0:
-            over_z(up, UP, UX)
-            arrived(kvw.at[:, 0], KVC)
-
-        w_pair = jnp.concatenate([kvw[i, j].reshape(512, 128) for i in range(4) for j in range(2)], axis=1)
-        pair = dot_nt(current, w_pair)
+            ff_to_x(down, DOWN, 1)
+            arrived(rkp.at[pl.ds(0, NZ - 1)], KPZ)
+            pieces = [
+                sum(pltpu.roll(rkp[4 * i + n].astype(F32), 32 * n, 1) for n in range(1, 4)) + rkp[4 * i].astype(F32)
+                for i in range(4)
+            ]
+            pair = jnp.concatenate(pieces, axis=1)
+        else:
+            w_pair = jnp.concatenate([kvw[i, j].reshape(512, 128) for i in range(4) for j in range(2)], axis=1)
+            pair = dot_nt(current, w_pair)
         row_head = lax.div(lax.broadcasted_iota(jnp.int32, (64, 256), 0), 16)
         lane_head = lax.div(lax.broadcasted_iota(jnp.int32, (64, 256), 1), 64)
         own_head = row_head == lane_head
@@ -360,8 +404,7 @@
             moved = pltpu.roll(steps[i // 8], (128 - ROWS * (i % 8)) % 128, 1)
             tzm[p, i] = jnp.sum(jnp.where(belongs, moved, 0.0), axis=0, keepdims=True)
 
-        @pl.loop(1, NZ)
-        def _(k):
+        for k in FAR_FIRST:
             zp, dev = dev_z(k)
             put(tzm.at[p, zp], rzm.at[p, z], base + RSZM, dev).start()
             put(tz.at[p, zp], rz.at[p, z], base + RSZ, dev).start()
@@ -369,8 +412,11 @@
         rz[p, z] = tz[p, z]
         rzm[p, z] = tzm[p, z]
         if p == 0:
-            over_z(down, DOWN, DX)
+            spread(wkv_ref, kvw.at[x, c, za, zc, y], KVZ, to_kv)
+            spread(wq_ref, qw.at[x, c, lax.rem(z, 4), y], QZ, to_q)
             to_core(ow, OX, OC)
+            ff_to_core(up, UP, 0)
+            ff_to_core(down, DOWN, 0)
 
         arrived(rzm.at[p, pl.ds(0, NZ - 1)], base + RSZM)
         stats = rzm[p].reshape(NZ, 128)
@@ -389,9 +435,8 @@
         for k in range(1, NY):
             put(att.at[p, y], att.at[p, y], base + GAY, dev_y(k)[1]).start()
         if p == 0:
+            ff_to_core(up, UP, 1)
             arrived(ow.at[:, 0], OC)
-            arrived(qw.at[0, 0], QZ)
-            to_x(qw, QX)
         arrived(att.at[p, pl.ds(0, 3)], base + GAY)
 
         w_o = jnp.concatenate([ow[i, j].reshape(256, 128) for i in range(4) for j in range(2)], axis=1)
@@ -399,25 +444,29 @@
         for k in range(1, NY):
             put(ob.at[p, y], ob.at[p, y], base + GOY, dev_y(k)[1]).start()
         if p == 0:
-            to_core(up, UX, UC)
+            ff_to_core(down, DOWN, 1)
+            arrived(kvw.at[0, 0], KVZ)
+            to_x(kvw, KVX)
+            arrived(qw.at[0, 0], QZ)
+            to_x(qw, QX)
         arrived(ob.at[p, pl.ds(0, 3)], base + GOY)
         residual = current.astype(F32) + jnp.concatenate([ob[p, i] for i in range(NY)], axis=1)
         settled = layer_norm(residual, ga_ref[...]).astype(BF)
 
         if p == 0:
-            arrived(up.at[:, 0], UC)
+            ff_ready(up, UP)
         w_u = jnp.concatenate([up[i, j].reshape(D, 128) for i in range(4) for j in range(2)], axis=1)
         product = dot_nt(settled, w_u)
         hidden = (0.5 * product * (1.0 + lax.erf(product * (0.5**0.5)))).astype(BF)
         if p == 0:
-            to_core(down, DX, DC)
-            arrived(down.at[:, 0], DC)
+            ff_ready(down, DOWN)
         w_d = jnp.concatenate([down[i, j].reshape(D, 128) for i in range(4) for j in range(2)], axis=1)
         fp[p, y] = dot_nn(hidden, w_d).astype(BF)
         for k in range(1, NY):
             put(fp.at[p, y], fp.at[p, y], base + RFY, dev_y(k)[1]).start()
         if p == 0:
             to_core(qw, QX, QC)
+            to_core(kvw, KVX, KVC)
             arrived(qw.at[:, 0], QC)
         arrived(fp.at[p, pl.ds(0, 3)], base + RFY)
         projected = fp[p, 0].astype(F32) + fp[p, 1].astype(F32) + fp[p, 2].astype(F32) + fp[p, 3].astype(F32)
@@ -470,12 +519,18 @@
     sent_but_own(qz, NZ, KVZ, to_kv == y)
     sent_but_own(hold, NZ, OZ, to_q == y)
     sent_but_own(hold, NZ, QZ, to_q == y)
-    for ref, xs, cs in ((qw, QX, QC), (kvw, KVX, KVC), (ow, OX, OC), (up, UX, UC), (down, DX, DC)):
+    sent_but_own(ws2, 8, WS2, to_p == t)
+    sent(rkp.at[pl.ds(0, NZ - 1)], KPZ)
+    for ref, xs, cs in ((qw, QX, QC), (kvw, KVX, KVC), (ow, OX, OC)):
         sent(ref.at[pl.ds(0, 3), 0], xs)
         sent(ref.at[:, 0], cs)
     for ph in (UP, DOWN):
         sent(up.at[0, 0, pl.ds(0, 8)], ph)
         sent(up.at[0, 0, pl.ds(0, 7)], ph + 3)
+        for n in range(2):
+            low, high = part(n)
+            sent(up.at[pl.ds(0, 3), 0, pl.ds(0, high - low)], ph + 4 + n)
+            sent(up.at[:, 0, pl.ds(0, high - low)], ph + 6 + n)
     for k in range(1, NY):
         sent(kvb.at[0], CY + k)
     sent(lim.at[pl.ds(0, 3)], LIM)
@@ -502,7 +557,7 @@
     result = pl.pallas_call(
         kernel,
         out_shape=jax.ShapeDtypeStruct((NZ, ROWS, D), BF),
-        in_specs=[smem, smem] + [pl.BlockSpec(memory_space=pl.ANY)] * 10,
+        in_specs=[smem, smem] + [pl.BlockSpec(memory_space=pltpu.HBM)] * 10,
         out_specs=pl.BlockSpec(memory_space=pltpu.VMEM),
         scratch_shapes=[
             pltpu.VMEM((TOK, D), BF),
@@ -513,6 +568,9 @@
             pltpu.VMEM((NY, 2, 144, KEYS), BF),
             pltpu.VMEM((NY, 8, 128), F32),
             pltpu.VMEM((8, 16, 128), BF),
+            pltpu.VMEM((8, 32, 128), BF),
+            pltpu.VMEM((NZ, ROWS, 128), BF),
+            pltpu.VMEM((NZ, ROWS, 128), BF),
             pltpu.VMEM((4, 2, 4, 4, 16, 128), BF),
             pltpu.VMEM((4, 2, 2, 2, 4, 32, 128), BF),
             pltpu.VMEM((4, 2, 4, 4, 16, 128), BF),
@@ -537,7 +595,7 @@
             pltpu.SemaphoreType.DMA((8,)),
         ],
         compiler_params=pltpu.CompilerParams(
-            collective_id=0, has_side_effects=True, vmem_limit_bytes=48 * 1024 * 1024
+            collective_id=0, has_side_effects=True, vmem_limit_bytes=63 * 1024 * 1024
         ),
     )(
         cache_len,

time: 152 us -> 137 us (0.901)
  the two profiles are of different devices: /device:TPU:32 before, /device:TPU:2 now
where the time goes in v3:
time: 137 us; the launch traced here: 136 us
  Pallas kernels  134 us (98%)
  local copies, waits for them, and re-layouts  1.87 us (1%)
    pallas_call x1, Pallas kernels, shards(): pl.pallas_call(kernel, out_shape=jax.ShapeDtypeStruct((NZ, ROWS, D), BF),...  134 us

profile of v3, /device:TPU:2, one launch (start us, length us, event | category | flops | bytes accessed | tf_op | source)
XLA Modules:
  0.0 136.3 jit_solution(2760306983126465827)
XLA Ops:
  0.7 133.8 %shard_map.118 = bf16[16,16,1024]{2,1,0:T(8,128)(2,1)} custom-call(s32[1]{0:T(128)S(6)} %copy.14.len_ref, s32[1,3]{1,0:T(1,128)} %page_ref.1, bf16[256,1024]{1,0:T(8,128)(2,1)} %bitcast.11, s32[2,1,256]{2,1,0:T(1,128)} %accept_hbm.1, bf16[3,128,2048]{2,1,0:T(8,128)(2,1)} %bitcast.10, bf16[16,128]{1,0:T(8,128)(2,1)} %bitcast.14, bf16[32,128]{1,0:T(8,128)(2,1)} %bitcast.13, ...), custom_call_target="tpu_custom_call" | custom-call | tf_op jit(solution)/shard_map/pallas_call | solution.py:557
  134.5 1.9 %copy.15 = bf16[1,256,1024]{2,1,0:T(8,128)(2,1)} copy(bf16[1,256,1024]{2,1,0:T(8,128)(2,1)} %bitcast.9) | data formatting | bytes 1048576

commit v4 on v3

--- a/solution.py
+++ b/solution.py
@@ -102,6 +102,41 @@
     def lanes(start, size):
         return pl.ds(pl.multiple_of(start, size), size)
 
+    barrier = pltpu.get_barrier_semaphore()
+    for k in range(8):
+        @pl.when((k > 0) | (from_t != t))
+        def _():
+            tell(dev_s(k, from_t))
+
+        @pl.when((k > 0) | (from_p != t))
+        def _():
+            tell(dev_s(k, from_p))
+    for k in range(1, NX):
+        tell(dev_x(k))
+    tell(partner)
+    for k in range(1, NY):
+        tell(dev_y(k)[1])
+
+    @pl.loop(1, NZ)
+    def _(k):
+        tell(dev_z(k)[1])
+
+    @pl.loop(0, NZ)
+    def _(i):
+        zs, ys = 8 * lax.div(i, 8) + 2 * y + lax.rem(lax.div(i, 4), 2), lax.rem(i, 4)
+
+        @pl.when((zs != z) | (ys != y))
+        def _():
+            tell({"seq": s, "tok": zs * NY + ys})
+
+    @pl.loop(0, NZ)
+    def _(i):
+        zs, ys = 4 * y + lax.div(i, 4), lax.rem(i, 4)
+
+        @pl.when((zs != z) | (ys != y))
+        def _():
+            tell({"seq": s, "tok": zs * NY + ys})
+
     local = [
         pltpu.make_async_copy(a, b, lsem.at[i])
         for i, (a, b) in enumerate(
@@ -120,41 +155,6 @@
     for copy in local:
         copy.start()
 
-    barrier = pltpu.get_barrier_semaphore()
-    for k in range(8):
-        @pl.when((k > 0) | (from_t != t))
-        def _():
-            tell(dev_s(k, from_t))
-
-        @pl.when((k > 0) | (from_p != t))
-        def _():
-            tell(dev_s(k, from_p))
-    for k in range(1, NX):
-        tell(dev_x(k))
-    tell(partner)
-    for k in range(1, NY):
-        tell(dev_y(k)[1])
-
-    @pl.loop(1, NZ)
-    def _(k):
-        tell(dev_z(k)[1])
-
-    @pl.loop(0, NZ)
-    def _(i):
-        zs, ys = 8 * lax.div(i, 8) + 2 * y + lax.rem(lax.div(i, 4), 2), lax.rem(i, 4)
-
-        @pl.when((zs != z) | (ys != y))
-        def _():
-            tell({"seq": s, "tok": zs * NY + ys})
-
-    @pl.loop(0, NZ)
-    def _(i):
-        zs, ys = 4 * y + lax.div(i, 4), lax.rem(i, 4)
-
-        @pl.when((zs != z) | (ys != y))
-        def _():
-            tell({"seq": s, "tok": zs * NY + ys})
-
     others = (to_t != t).astype(jnp.int32) + (to_kv != y).astype(jnp.int32) + (to_q != y).astype(jnp.int32)
     others += (to_p != t).astype(jnp.int32)
     pl.semaphore_wait(barrier, 14 + NX + (NY - 1) + 3 * (NZ - 1) + others)
@@ -271,7 +271,6 @@
         zp, dev = dev_z(k)
         put(kp.at[zp], rkp.at[z], KPZ, dev).start()
     rkp[z] = kp[z]
-    spread(wo_ref, ow.at[x, c, lax.rem(z, 4), y], OZ, to_q)
 
     vt[:, :, 128:144, :] = jnp.ones((NY, 2, 16, KEYS), BF)
 
@@ -308,20 +307,16 @@
 
             for k in FAR_FIRST:
                 put(qz.at[z], qz.at[z], base + GQZ, dev_z(k)[1]).start()
-            arrived(kvw.at[:, 0], KVC)
             arrived(qz.at[pl.ds(0, NZ - 1)], base + GQZ)
+            to_core(kvw, KVX, KVC)
             qt[1] = jnp.transpose(qz[...].reshape(TOK, 256)).reshape(NZ, 16, TOK)
         else:
             arrived(qt.at[p, pl.ds(0, NZ - 1)], base + GQZ)
+            spread(wo_ref, ow.at[x, c, lax.rem(z, 4), y], OZ, to_q)
 
         @pl.loop(0, NY)
         def _(j):
             if p == 0:
-                @pl.when(j == 1)
-                def _():
-                    arrived(ow.at[0, 0], OZ)
-                    to_x(ow, OX)
-
                 @pl.when(j == 3)
                 def _():
                     ff_to_x(up, UP, 1)
@@ -369,6 +364,7 @@
             ]
             pair = jnp.concatenate(pieces, axis=1)
         else:
+            arrived(kvw.at[:, 0], KVC)
             w_pair = jnp.concatenate([kvw[i, j].reshape(512, 128) for i in range(4) for j in range(2)], axis=1)
             pair = dot_nt(current, w_pair)
         row_head = lax.div(lax.broadcasted_iota(jnp.int32, (64, 256), 0), 16)
@@ -412,9 +408,8 @@
         rz[p, z] = tz[p, z]
         rzm[p, z] = tzm[p, z]
         if p == 0:
-            spread(wkv_ref, kvw.at[x, c, za, zc, y], KVZ, to_kv)
-            spread(wq_ref, qw.at[x, c, lax.rem(z, 4), y], QZ, to_q)
-            to_core(ow, OX, OC)
+            arrived(ow.at[0, 0], OZ)
+            to_x(ow, OX)
             ff_to_core(up, UP, 0)
             ff_to_core(down, DOWN, 0)
 
@@ -424,6 +419,10 @@
         share = scale_z / jnp.sum(scale_z * pltpu.roll(stats, 64, 1), axis=0, keepdims=True)
         share = jnp.transpose(jnp.concatenate([share, jnp.zeros((128 - NZ, 128), F32)], axis=0))
         arrived(rz.at[p, pl.ds(0, NZ - 1)], base + RSZ)
+        if p == 0:
+            spread(wq_ref, qw.at[x, c, lax.rem(z, 4), y], QZ, to_q)
+            spread(wkv_ref, kvw.at[x, c, za, zc, y], KVZ, to_kv)
+            to_core(ow, OX, OC)
         lower = lax.broadcasted_iota(jnp.int32, (ROWS, 128), 1) < 64
         halves = [jnp.zeros((ROWS, 128), F32), jnp.zeros((ROWS, 128), F32)]
         for i in range(NZ):
@@ -445,8 +444,6 @@
             put(ob.at[p, y], ob.at[p, y], base + GOY, dev_y(k)[1]).start()
         if p == 0:
             ff_to_core(down, DOWN, 1)
-            arrived(kvw.at[0, 0], KVZ)
-            to_x(kvw, KVX)
             arrived(qw.at[0, 0], QZ)
             to_x(qw, QX)
         arrived(ob.at[p, pl.ds(0, 3)], base + GOY)
@@ -466,7 +463,8 @@
             put(fp.at[p, y], fp.at[p, y], base + RFY, dev_y(k)[1]).start()
         if p == 0:
             to_core(qw, QX, QC)
-            to_core(kvw, KVX, KVC)
+            arrived(kvw.at[0, 0], KVZ)
+            to_x(kvw, KVX)
             arrived(qw.at[:, 0], QC)
         arrived(fp.at[p, pl.ds(0, 3)], base + RFY)
         projected = fp[p, 0].astype(F32) + fp[p, 1].astype(F32) + fp[p, 2].astype(F32) + fp[p, 3].astype(F32)

time: 137 us -> 131 us (0.956)
  the two profiles are of different devices: /device:TPU:2 before, /device:TPU:8 now
where the time goes in v4:
time: 131 us
  Pallas kernels  129 us (98%)
  local copies, waits for them, and re-layouts  1.87 us (1%)
    pallas_call x1, Pallas kernels, shards(): pl.pallas_call(kernel, out_shape=jax.ShapeDtypeStruct((NZ, ROWS, D), BF),...  129 us

profile of v4, /device:TPU:8, one launch (start us, length us, event | category | flops | bytes accessed | tf_op | source)
XLA Modules:
  0.0 131.2 jit_solution(4065109381549943020)
XLA Ops:
  0.7 128.7 %shard_map.118 = bf16[16,16,1024]{2,1,0:T(8,128)(2,1)} custom-call(s32[1]{0:T(128)S(6)} %copy.14.len_ref, s32[1,3]{1,0:T(1,128)} %page_ref.1, bf16[256,1024]{1,0:T(8,128)(2,1)} %bitcast.11, s32[2,1,256]{2,1,0:T(1,128)} %accept_hbm.1, bf16[3,128,2048]{2,1,0:T(8,128)(2,1)} %bitcast.10, bf16[16,128]{1,0:T(8,128)(2,1)} %bitcast.14, bf16[32,128]{1,0:T(8,128)(2,1)} %bitcast.13, ...), custom_call_target="tpu_custom_call" | custom-call | tf_op jit(solution)/shard_map/pallas_call | solution.py:555
  129.3 1.9 %copy.15 = bf16[1,256,1024]{2,1,0:T(8,128)(2,1)} copy(bf16[1,256,1024]{2,1,0:T(8,128)(2,1)} %bitcast.9) | data formatting | bytes 1048576

commit v5 on v4

--- a/solution.py
+++ b/solution.py
@@ -18,10 +18,10 @@
 FLOOR_SCORE = -1e30
 MASKED = -3e38
 
-(WS, KVZ, OZ, QZ, KVX, OX, QX, KVC, OC, QC, WS2, KPZ, LIM) = range(13)
-CY = 13
-UP, DOWN = 17, 25
-PASS = 33
+(WS, KVZ, OZ, QZ, KVX, OX, QX, KVC, OC, QC, WS2, KPZ, LIM, OY) = range(14)
+CY = 14
+UP, DOWN = 18, 26
+PASS = 34
 FAR_FIRST = (8, 7, 9, 6, 10, 5, 11, 4, 12, 3, 13, 2, 14, 1, 15)
 (GQZ, RSZ, RSZM, GAY, GOY, RFY) = range(6)
 FIN_Y, FIN_Z = PASS + 12, PASS + 12
@@ -75,6 +75,7 @@
     def dev_x(k):
         return {"seq": lax.rem(x + k, NX) * 2 + c, "tok": t}
 
+    ow_own = ow.at[:, :, y]
     partner = {"seq": x * 2 + 1 - c, "tok": t}
 
     def put(src, dst, ph, dev, rph=None):
@@ -254,8 +255,8 @@
         arrived(ref.at[pl.ds(0, 3), 0], xs)
         put(ref.at[:, c], ref.at[:, c], cs, partner).start()
 
+    spread(wo_ref, ow.at[x, c, to_q, lax.rem(z, 4), y], OZ, to_q)
     direct(wu_ref, up, UP)
-    direct(wd_ref, down, DOWN)
     arrived(ws, WS)
     local[0].wait()
     wq_cols = jnp.concatenate([ws[i] for i in range(8)], axis=1)
@@ -271,6 +272,7 @@
         zp, dev = dev_z(k)
         put(kp.at[zp], rkp.at[z], KPZ, dev).start()
     rkp[z] = kp[z]
+    direct(wd_ref, down, DOWN)
 
     vt[:, :, 128:144, :] = jnp.ones((NY, 2, 16, KEYS), BF)
 
@@ -282,12 +284,10 @@
     local[1].wait()
     local[2].wait()
     turn(y)
+    arrived(ow.at[0, 0, 0], OZ)
+    to_x(ow_own, OX)
     local[3].wait()
     local[4].wait()
-    relay(up, UP)
-    ff_to_x(up, UP, 0)
-    relay(down, DOWN)
-    ff_to_x(down, DOWN, 0)
     for k in (1, 3, 2):
         src = lax.rem(y + NY - k, NY)
         arrived(kvb.at[src], CY + k)
@@ -302,6 +302,8 @@
     for p in range(2):
         base = PASS + 6 * p
         if p == 1:
+            for k in range(1, NY):
+                put(ow_own, ow_own, OY, dev_y(k)[1]).start()
             w_q = jnp.concatenate([qw[i, j].reshape(256, 128) for i in range(4) for j in range(2)], axis=1)
             qz[z] = dot_nt(current, w_q).astype(BF) * jnp.asarray(0.125, BF)
 
@@ -312,14 +314,17 @@
             qt[1] = jnp.transpose(qz[...].reshape(TOK, 256)).reshape(NZ, 16, TOK)
         else:
             arrived(qt.at[p, pl.ds(0, NZ - 1)], base + GQZ)
-            spread(wo_ref, ow.at[x, c, lax.rem(z, 4), y], OZ, to_q)
+            relay(up, UP)
+            ff_to_x(up, UP, 0)
+            spread(wq_ref, qw.at[x, c, lax.rem(z, 4), y], QZ, to_q)
 
         @pl.loop(0, NY)
         def _(j):
             if p == 0:
-                @pl.when(j == 3)
+                @pl.when(j == 1)
                 def _():
-                    ff_to_x(up, UP, 1)
+                    relay(down, DOWN)
+                    ff_to_x(down, DOWN, 0)
 
             for i in range(2):
                 keys = kvb[j, 0, :, :, 128 * i : 128 * i + 128].reshape(KEYS, 128)
@@ -356,7 +361,6 @@
                 pm[j, 5 + 2 * i : 6 + 2 * i, :] = summed[128:129, TOK : 2 * TOK]
 
         if p == 0:
-            ff_to_x(down, DOWN, 1)
             arrived(rkp.at[pl.ds(0, NZ - 1)], KPZ)
             pieces = [
                 sum(pltpu.roll(rkp[4 * i + n].astype(F32), 32 * n, 1) for n in range(1, 4)) + rkp[4 * i].astype(F32)
@@ -408,8 +412,8 @@
         rz[p, z] = tz[p, z]
         rzm[p, z] = tzm[p, z]
         if p == 0:
-            arrived(ow.at[0, 0], OZ)
-            to_x(ow, OX)
+            ff_to_x(up, UP, 1)
+            ff_to_x(down, DOWN, 1)
             ff_to_core(up, UP, 0)
             ff_to_core(down, DOWN, 0)
 
@@ -420,9 +424,8 @@
         share = jnp.transpose(jnp.concatenate([share, jnp.zeros((128 - NZ, 128), F32)], axis=0))
         arrived(rz.at[p, pl.ds(0, NZ - 1)], base + RSZ)
         if p == 0:
-            spread(wq_ref, qw.at[x, c, lax.rem(z, 4), y], QZ, to_q)
             spread(wkv_ref, kvw.at[x, c, za, zc, y], KVZ, to_kv)
-            to_core(ow, OX, OC)
+            to_core(ow_own, OX, OC)
         lower = lax.broadcasted_iota(jnp.int32, (ROWS, 128), 1) < 64
         halves = [jnp.zeros((ROWS, 128), F32), jnp.zeros((ROWS, 128), F32)]
         for i in range(NZ):
@@ -435,20 +438,25 @@
             put(att.at[p, y], att.at[p, y], base + GAY, dev_y(k)[1]).start()
         if p == 0:
             ff_to_core(up, UP, 1)
-            arrived(ow.at[:, 0], OC)
+            arrived(ow.at[:, 0, 0], OC)
         arrived(att.at[p, pl.ds(0, 3)], base + GAY)
 
-        w_o = jnp.concatenate([ow[i, j].reshape(256, 128) for i in range(4) for j in range(2)], axis=1)
-        ob[p, y] = dot_nt(jnp.concatenate([att[p, i] for i in range(NY)], axis=1), w_o)
-        for k in range(1, NY):
-            put(ob.at[p, y], ob.at[p, y], base + GOY, dev_y(k)[1]).start()
-        if p == 0:
+        heads = jnp.concatenate([att[p, i] for i in range(NY)], axis=1)
+        if p == 0:
+            w_o = jnp.concatenate([ow[i, j, y].reshape(256, 128) for i in range(4) for j in range(2)], axis=1)
+            ob[y] = dot_nt(heads, w_o)
+            for k in range(1, NY):
+                put(ob.at[y], ob.at[y], base + GOY, dev_y(k)[1]).start()
             ff_to_core(down, DOWN, 1)
             arrived(qw.at[0, 0], QZ)
             to_x(qw, QX)
-        arrived(ob.at[p, pl.ds(0, 3)], base + GOY)
-        residual = current.astype(F32) + jnp.concatenate([ob[p, i] for i in range(NY)], axis=1)
-        settled = layer_norm(residual, ga_ref[...]).astype(BF)
+            arrived(ob.at[pl.ds(0, 3)], base + GOY)
+            projected = jnp.concatenate([ob[i] for i in range(NY)], axis=1)
+        else:
+            arrived(ow.at[:, :, pl.ds(0, 3)], OY)
+            w_o = jnp.concatenate([ow[i, j].reshape(D, 128) for i in range(4) for j in range(2)], axis=1)
+            projected = dot_nt(heads, w_o)
+        settled = layer_norm(current.astype(F32) + projected, ga_ref[...]).astype(BF)
 
         if p == 0:
             ff_ready(up, UP)
@@ -519,7 +527,8 @@
     sent_but_own(hold, NZ, QZ, to_q == y)
     sent_but_own(ws2, 8, WS2, to_p == t)
     sent(rkp.at[pl.ds(0, NZ - 1)], KPZ)
-    for ref, xs, cs in ((qw, QX, QC), (kvw, KVX, KVC), (ow, OX, OC)):
+    sent(ow.at[:, :, pl.ds(0, 3)], OY)
+    for ref, xs, cs in ((qw, QX, QC), (kvw, KVX, KVC), (ow_own, OX, OC)):
         sent(ref.at[pl.ds(0, 3), 0], xs)
         sent(ref.at[:, 0], cs)
     for ph in (UP, DOWN):
@@ -538,7 +547,8 @@
         sent(rz.at[p, pl.ds(0, NZ - 1)], base + RSZ)
         sent(rzm.at[p, pl.ds(0, NZ - 1)], base + RSZM)
         sent(att.at[p, pl.ds(0, 3)], base + GAY)
-        sent(ob.at[p, pl.ds(0, 3)], base + GOY)
+        if p == 0:
+            sent(ob.at[pl.ds(0, 3)], base + GOY)
         sent(fp.at[p, pl.ds(0, 3)], base + RFY)
 
     @pl.loop(1, NZ)
@@ -571,7 +581,7 @@
             pltpu.VMEM((NZ, ROWS, 128), BF),
             pltpu.VMEM((4, 2, 4, 4, 16, 128), BF),
             pltpu.VMEM((4, 2, 2, 2, 4, 32, 128), BF),
-            pltpu.VMEM((4, 2, 4, 4, 16, 128), BF),
+            pltpu.VMEM((4, 2, NY, 4, 4, 16, 128), BF),
             pltpu.VMEM((4, 2, NZ, 64, 128), BF),
             pltpu.VMEM((4, 2, NZ, 64, 128), BF),
             pltpu.VMEM((NZ, 16, 128), BF),
@@ -584,7 +594,7 @@
             pltpu.VMEM((2, NZ, ROWS, 256), BF),
             pltpu.VMEM((2, NZ, 1, 128), F32),
             pltpu.VMEM((2, NY, ROWS, 256), BF),
-            pltpu.VMEM((2, NY, ROWS, 256), F32),
+            pltpu.VMEM((NY, ROWS, 256), F32),
             pltpu.VMEM((2, NY, ROWS, D), BF),
             pltpu.VMEM((ROWS, D), BF),
             pltpu.VMEM((NZ, ROWS, 256), BF),

time: 131 us -> 125 us (0.954)
  the two profiles are of different devices: /device:TPU:8 before, /device:TPU:2 now
where the time goes in v5:
time: 125 us
  Pallas kernels  122 us (98%)
  local copies, waits for them, and re-layouts  1.87 us (1%)
    pallas_call x1, Pallas kernels, shards(): pl.pallas_call(kernel, out_shape=jax.ShapeDtypeStruct((NZ, ROWS, D), BF),...  122 us

profile of v5, /device:TPU:2, one launch (start us, length us, event | category | flops | bytes accessed | tf_op | source)
XLA Modules:
  0.0 124.9 jit_solution(11011586268938670204)
XLA Ops:
  0.7 122.4 %shard_map.118 = bf16[16,16,1024]{2,1,0:T(8,128)(2,1)} custom-call(s32[1]{0:T(128)S(6)} %copy.14.len_ref, s32[1,3]{1,0:T(1,128)} %page_ref.1, bf16[256,1024]{1,0:T(8,128)(2,1)} %bitcast.11, s32[2,1,256]{2,1,0:T(1,128)} %accept_hbm.1, bf16[3,128,2048]{2,1,0:T(8,128)(2,1)} %bitcast.10, bf16[16,128]{1,0:T(8,128)(2,1)} %bitcast.14, bf16[32,128]{1,0:T(8,128)(2,1)} %bitcast.13, ...), custom_call_target="tpu_custom_call" | custom-call | tf_op jit(solution)/shard_map/pallas_call | solution.py:565
  123.0 1.9 %copy.15 = bf16[1,256,1024]{2,1,0:T(8,128)(2,1)} copy(bf16[1,256,1024]{2,1,0:T(8,128)(2,1)} %bitcast.9) | data formatting | bytes 1048576

commit v6 on v5

--- a/solution.py
+++ b/solution.py
@@ -309,8 +309,11 @@
 
             for k in FAR_FIRST:
                 put(qz.at[z], qz.at[z], base + GQZ, dev_z(k)[1]).start()
+            to_core(kvw, KVX, KVC)
+            arrived(kvw.at[:, 0], KVC)
+            w_pair = jnp.concatenate([kvw[i, j].reshape(512, 128) for i in range(4) for j in range(2)], axis=1)
+            pair = dot_nt(current, w_pair)
             arrived(qz.at[pl.ds(0, NZ - 1)], base + GQZ)
-            to_core(kvw, KVX, KVC)
             qt[1] = jnp.transpose(qz[...].reshape(TOK, 256)).reshape(NZ, 16, TOK)
         else:
             arrived(qt.at[p, pl.ds(0, NZ - 1)], base + GQZ)
@@ -367,10 +370,6 @@
                 for i in range(4)
             ]
             pair = jnp.concatenate(pieces, axis=1)
-        else:
-            arrived(kvw.at[:, 0], KVC)
-            w_pair = jnp.concatenate([kvw[i, j].reshape(512, 128) for i in range(4) for j in range(2)], axis=1)
-            pair = dot_nt(current, w_pair)
         row_head = lax.div(lax.broadcasted_iota(jnp.int32, (64, 256), 0), 16)
         lane_head = lax.div(lax.broadcasted_iota(jnp.int32, (64, 256), 1), 64)
         own_head = row_head == lane_head

time: 125 us -> 125 us (level)
  no operation moved by 1% of the time
where the time goes in v6:
time: 125 us
  Pallas kernels  122 us (98%)
  local copies, waits for them, and re-layouts  1.87 us (1%)
    pallas_call x1, Pallas kernels, shards(): pl.pallas_call(kernel, out_shape=jax.ShapeDtypeStruct((NZ, ROWS, D), BF),...  122 us

profile of v6, /device:TPU:2, one launch (start us, length us, event | category | flops | bytes accessed | tf_op | source)
XLA Modules:
  0.0 125.0 jit_solution(10621868439578304848)
XLA Ops:
  0.7 122.4 %shard_map.118 = bf16[16,16,1024]{2,1,0:T(8,128)(2,1)} custom-call(s32[1]{0:T(128)S(6)} %copy.14.len_ref, s32[1,3]{1,0:T(1,128)} %page_ref.1, bf16[256,1024]{1,0:T(8,128)(2,1)} %bitcast.11, s32[2,1,256]{2,1,0:T(1,128)} %accept_hbm.1, bf16[3,128,2048]{2,1,0:T(8,128)(2,1)} %bitcast.10, bf16[16,128]{1,0:T(8,128)(2,1)} %bitcast.14, bf16[32,128]{1,0:T(8,128)(2,1)} %bitcast.13, ...), custom_call_target="tpu_custom_call" | custom-call | tf_op jit(solution)/shard_map/pallas_call | solution.py:564
  123.1 1.9 %copy.15 = bf16[1,256,1024]{2,1,0:T(8,128)(2,1)} copy(bf16[1,256,1024]{2,1,0:T(8,128)(2,1)} %bitcast.9) | data formatting | bytes 1048576
